TPU v7x, 256 devices: a whole 4x4x8 slice. The times are simulated.
256 devices in a mesh: sky: 64 (over z, x, core), grp: 4 (over y).
Axes of the slice: x: 4, y: 4, z: 8, core: 2. Of those that a mesh axis runs over, the one named last changes fastest.
Arguments:
- sky_strip: float32 [64, 32768], P(None, 'sky'), may hold values from -6 to 6
- exposures: float32 [1024, 64, 2048], P(('sky', 'grp')), may hold values from -6 to 6
- psf_taps: float32 [1024, 256], P(('sky', 'grp')), may hold values from -0.375 to 0.375
- offsets: int32 [1024], P(('sky', 'grp')), may hold values from 0 to 511
- counts: int32 [256], P(('sky', 'grp')), may hold values from 1 to 4, as said below
- features: bfloat16 [128, 64, 32768], P(None, None, 'sky'), may hold values from -6 to 6
- conv_weight: bfloat16 [128, 3, 3, 128], P('grp'), may hold values from -0.1875 to 0.1875
- conv_bias: float32 [128], P('grp'), may hold values from -4 to 4
- out_weight: float32 [128], P('grp'), may hold values from -0.5 to 0.5
Outputs:
- score_map: float32 [64, 32768], P('grp', 'sky')
Inputs may be any that keep to these rules, and one draw needn't show every extreme that they name: Slots 0 to counts[d] - 1 of device d hold exposures; some device uses all 4 slots and some only one.
All inputs are finite; a program needn't handle non-finite values.
Results may differ from a plain program's by a relative error of at most 0.0003.
Values may be sent and summed in bfloat16 or wider, within the bound.
No kernel may reach another device: no remote copies, remote signals or barrier semaphores. Data moves between devices by JAX's collectives and lax.ppermute only.
A program may use at most 128 MiB of HBM per device.

v0:
```python
import functools

import jax
import jax.numpy as jnp
from jax import lax
from jax.experimental import pallas as pl
from jax.experimental.pallas import tpu as pltpu
from jax.sharding import PartitionSpec as P

F32 = jnp.float32
BF16 = jnp.bfloat16
LANES = 128


def shifted(x, axis, by):
    length = lax.axis_size(axis)
    return lax.ppermute(x, axis, [(i, (i + by) % length) for i in range(length)])


def partner(x, axis, mask):
    return lax.ppermute(x, axis, [(i, i ^ mask) for i in range(lax.axis_size(axis))])


def lane_index(shape):
    return lax.broadcasted_iota(jnp.int32, shape, 1)


def column(row):
    n = row.shape[1]
    spread = jnp.broadcast_to(row, (n, n))
    diagonal = lax.broadcasted_iota(jnp.int32, (n, n), 0) == lane_index((n, n))
    return jnp.sum(jnp.where(diagonal, spread, 0.0), axis=1, keepdims=True)


def weighted_silu(hidden, half_weight):
    return hidden * (1.0 + jnp.tanh(0.5 * hidden)) * half_weight


def conv_kernel(w_ref, bias_ref, ow_ref, x_ref, prior_ref, left_ref, right_ref, t_ref, p_ref, carry_ref):
    step = pl.program_id(0)
    channels, rows, cols = x_ref.shape
    outs = bias_ref.shape[1]
    taps = 3 * outs
    depth = channels * rows

    @pl.when(step == 0)
    def _():
        repeat = jnp.where(
            lane_index((channels, depth)) // rows == lax.broadcasted_iota(jnp.int32, (channels, depth), 0), 1.0, 0.0
        ).astype(BF16)
        spread = jnp.dot(w_ref[...], repeat, preferred_element_type=F32)
        row_in = lane_index((taps, depth)) % rows
        for j in range(rows + 2):
            band = jnp.zeros((taps, depth), F32)
            for a in range(3):
                band = jnp.where(row_in == j - 2 + a, spread[a * taps : (a + 1) * taps], band)
            t_ref[j * taps : (j + 1) * taps, :] = band.astype(BF16)
        carry_ref[...] = jnp.zeros_like(carry_ref)
        left_ref[...] = jnp.zeros_like(left_ref)
        right_ref[...] = jnp.zeros_like(right_ref)

    @pl.when(step > 0)
    def _():
        carry_ref[...] = p_ref[rows * taps :, :]

    x = x_ref[...].reshape(depth, cols)
    p_ref[...] = jnp.dot(t_ref[...], x, preferred_element_type=F32)

    bias = column(bias_ref[...])
    half_weight = column(ow_ref[...]) * 0.5
    lane = lane_index((1, LANES))
    col = lane_index((1, cols))
    inner = jnp.logical_and(col > 0, col < cols - 1)

    def one_row(i, carried):
        row = step * rows - 1 + i
        parts = []
        for b in range(3):
            part = p_ref[i * taps + b * outs : i * taps + (b + 1) * outs, :]
            if carried:
                part = part + carry_ref[i * taps + b * outs : i * taps + (b + 1) * outs, :]
            parts.append(part)
        before, here, after = parts
        hidden = pltpu.roll(before, 1, 1) + here + pltpu.roll(after, cols - 1, 1) + bias
        score = jnp.sum(weighted_silu(hidden, half_weight), axis=0, keepdims=True)
        prior_ref[pl.ds(row, 1), :] = jnp.where(inner, score, 0.0)
        mine = (lane >> 1) == row
        tail = before[:, cols - LANES :] + jnp.where(
            lane == LANES - 2, pltpu.roll(here[:, cols - LANES :], LANES - 1, 1), 0.0
        )
        left_ref[...] += jnp.where(mine, pltpu.roll(tail, 2 * row + 2, 1), 0.0)
        head = after[:, :LANES] + jnp.where(lane == 1, pltpu.roll(here[:, :LANES], 1, 1), 0.0)
        right_ref[...] += jnp.where(mine, pltpu.roll(head, 2 * row, 1), 0.0)

    @pl.when(step > 0)
    def _():
        one_row(0, True)

    for i in range(1, rows):
        one_row(i, i < 2)

    @pl.when(step == pl.num_programs(0) - 1)
    def _():
        one_row(rows, False)


def conv_prior(features, weight, bias, out_weight):
    channels, strip_rows, cols = features.shape
    outs = bias.shape[0]
    rows = 8
    taps = 3 * outs
    flat = weight.transpose(1, 2, 0, 3).reshape(9 * outs, channels)
    full = lambda shape: pl.BlockSpec(shape, lambda i: (0,) * len(shape))
    return pl.pallas_call(
        conv_kernel,
        grid=(strip_rows // rows,),
        in_specs=[
            full((9 * outs, channels)),
            full((1, outs)),
            full((1, outs)),
            pl.BlockSpec((channels, rows, cols), lambda i: (0, i, 0)),
        ],
        out_specs=[full((strip_rows, cols)), full((outs, LANES)), full((outs, LANES))],
        out_shape=[
            jax.ShapeDtypeStruct((strip_rows, cols), F32),
            jax.ShapeDtypeStruct((outs, LANES), F32),
            jax.ShapeDtypeStruct((outs, LANES), F32),
        ],
        scratch_shapes=[
            pltpu.VMEM(((rows + 2) * taps, channels * rows), BF16),
            pltpu.VMEM(((rows + 2) * taps, cols), F32),
            pltpu.VMEM((2 * taps, cols), F32),
        ],
        compiler_params=pltpu.CompilerParams(vmem_limit_bytes=40 << 20),
        cost_estimate=pl.CostEstimate(flops=8_000_000_000, bytes_accessed=9_000_000, transcendentals=1_000_000),
    )(flat, bias.reshape(1, outs), out_weight.reshape(1, outs), features)


def split(x):
    high = x.astype(BF16)
    return high, (x - high.astype(F32)).astype(BF16)


def exposure_kernel(
    offsets_ref, counts_ref, group_ref, s0, s1, s2, s3, s4, record_ref, taps_ref, prior_ref, left_ref, right_ref,
    bias_ref, ow_ref, o0, o1, o2, o3, ext_ref, acc_ref,
):
    slot = pl.program_id(0)
    rows, cols = s0.shape
    width = record_ref.shape[2]
    tap_count = taps_ref.shape[2]
    pieces = width // tap_count
    tiles = width // LANES

    @pl.when(slot == 0)
    def _():
        for d, part in enumerate((s0, s1, s2, s3, s4)):
            ext_ref[:, d * cols : (d + 1) * cols] = part[...]
        acc_ref[:, cols:] = jnp.zeros((rows, acc_ref.shape[1] - cols), F32)
        acc_ref[:, :cols] = prior_ref[...]
        edge = left_ref[...] + right_ref[...] + column(bias_ref[...])
        score = jnp.sum(weighted_silu(edge, column(ow_ref[...]) * 0.5), axis=0, keepdims=True)
        lane = lane_index((rows, LANES))
        own = jnp.where((lane >> 1) == lax.broadcasted_iota(jnp.int32, (rows, LANES), 0), score, 0.0)
        last = jnp.sum(jnp.where((lane & 1) == 0, own, 0.0), axis=1, keepdims=True)
        following = jnp.sum(jnp.where((lane & 1) == 1, own, 0.0), axis=1, keepdims=True)
        acc_ref[:, cols - LANES : cols] += jnp.where(lane == LANES - 1, last, 0.0)
        acc_ref[:, cols : cols + LANES] += jnp.where(lane == 0, following, 0.0)

    @pl.when(slot < counts_ref[0])
    def _():
        offset = offsets_ref[slot]
        rest = offset % LANES
        base = pl.multiple_of(offset - rest, LANES)
        lane = lane_index((rows, LANES))

        taps = taps_ref[0]
        wide = jnp.concatenate([taps, jnp.zeros_like(taps)], axis=1)
        band = pltpu.roll(jnp.broadcast_to(wide, (tap_count, 2 * tap_count)), 0, 1, stride=1, stride_axis=0)
        band_high, band_low = split(band)

        turned = [
            pltpu.roll(ext_ref[:, pl.ds(base + m * LANES, LANES)], LANES - rest, 1) for m in range(tiles + 1)
        ]
        keep = lane < LANES - rest
        window = [jnp.where(keep, turned[m], turned[m + 1]) for m in range(tiles)]
        per = tap_count // LANES

        def stacked(parts):
            return jnp.concatenate(
                [jnp.concatenate(parts[n * per : (n + 1) * per], axis=1) for n in range(pieces)], axis=0
            )

        def product(x, matrix, dims):
            return lax.dot_general(x, matrix, (dims, ((), ())), preferred_element_type=F32)

        def banded(x, shift, dims):
            high, low = split(x)
            total = None
            for at, columns in ((0, 0), (shift, 1)):
                cut = slice(columns * tap_count, (columns + 1) * tap_count)
                x_high, x_low = high, low
                if at:
                    k = (at * rows) % x.shape[0]
                    x_high = jnp.concatenate([high[k:], high[:k]], axis=0)
                    x_low = jnp.concatenate([low[k:], low[:k]], axis=0)
                part = (
                    product(x_high, band_high[:, cut], dims)
                    + product(x_low, band_high[:, cut], dims)
                    + product(x_high, band_low[:, cut], dims)
                )
                total = part if total is None else total + part
            return total

        model = banded(stacked(window), pieces - 1, ((1,), (0,)))
        record = record_ref[0]
        residual = (
            jnp.concatenate([record[:, n * tap_count : (n + 1) * tap_count] for n in range(pieces)], axis=0) - model
        )
        back = banded(residual, 1, ((1,), (1,)))
        moved = []
        for m in range(tiles):
            n, h = divmod(m, per)
            moved.append(pltpu.roll(back[n * rows : (n + 1) * rows, h * LANES : (h + 1) * LANES], rest, 1))
        nothing = jnp.zeros((rows, LANES), F32)
        spill = lane < rest
        for m in range(tiles + 1):
            inside = moved[m] if m < tiles else nothing
            earlier = moved[m - 1] if m > 0 else nothing
            acc_ref[:, pl.ds(base + m * LANES, LANES)] += jnp.where(spill, earlier, inside)

    @pl.when(slot == pl.num_programs(0) - 1)
    def _():
        share = o0.shape[0]
        for k, out in enumerate((o0, o1, o2, o3)):
            first = pl.multiple_of((group_ref[0] ^ k) * share, share)
            out[...] = acc_ref[pl.ds(first, share), :]


def exposure_terms(group, offsets, counts, sky_parts, exposures, psf_taps, prior, left, right, bias, out_weight, n_grp):
    slots, rows, width = exposures.shape
    cols = sky_parts[0].shape[1]
    reach = len(sky_parts) * cols
    outs = bias.shape[0]
    share = rows // n_grp
    full = lambda shape: pl.BlockSpec(shape, lambda i, *_: (0,) * len(shape))
    return pl.pallas_call(
        exposure_kernel,
        grid_spec=pltpu.PrefetchScalarGridSpec(
            num_scalar_prefetch=3,
            grid=(slots,),
            in_specs=[full((rows, cols))] * len(sky_parts)
            + [
                pl.BlockSpec((1, rows, width), lambda i, *_: (i, 0, 0)),
                pl.BlockSpec((1, 1, psf_taps.shape[1]), lambda i, *_: (i, 0, 0)),
                full((rows, cols)),
                full((outs, LANES)),
                full((outs, LANES)),
                full((1, outs)),
                full((1, outs)),
            ],
            out_specs=[full((share, reach))] * n_grp,
            scratch_shapes=[pltpu.VMEM((rows, reach), F32), pltpu.VMEM((rows, reach), F32)],
        ),
        out_shape=[jax.ShapeDtypeStruct((share, reach), F32)] * n_grp,
        compiler_params=pltpu.CompilerParams(vmem_limit_bytes=40 << 20),
        cost_estimate=pl.CostEstimate(flops=4_000_000_000, bytes_accessed=4_000_000, transcendentals=0),
    )(
        offsets, counts, group, *sky_parts, exposures, psf_taps.reshape(slots, 1, -1), prior, left, right,
        bias.reshape(1, outs), out_weight.reshape(1, outs),
    )


def sum_kernel(a, b, c, d, *outs):
    total = a[...] + b[...] + c[...] + d[...]
    cols = outs[0].shape[1]
    for k, out in enumerate(outs):
        out[...] = total[:, k * cols : (k + 1) * cols]


def on_device(
    sky_strip, exposures, psf_taps, offsets, counts, features, conv_weight, conv_bias, out_weight
):
    n_grp = lax.axis_size("grp")
    cols = sky_strip.shape[1]
    reach_blocks = exposures.shape[2] // cols
    parts = [sky_strip]
    for distance in range(1, reach_blocks + 1):
        parts.append(shifted(sky_strip, "sky", -distance))
    prior, left, right = conv_prior(features, conv_weight, conv_bias, out_weight)
    right = shifted(right, "sky", -1)
    group = lax.axis_index("grp").astype(jnp.int32).reshape(1)
    terms = exposure_terms(
        group, offsets, counts, parts, exposures, psf_taps, prior, left, right, conv_bias, out_weight, n_grp
    )
    received = [terms[0]] + [partner(terms[k], "grp", k) for k in range(1, n_grp)]
    share = terms[0].shape[0]
    pieces = pl.pallas_call(
        sum_kernel,
        out_shape=[jax.ShapeDtypeStruct((share, cols), F32)] * (reach_blocks + 1),
        cost_estimate=pl.CostEstimate(flops=200_000, bytes_accessed=1_000_000, transcendentals=0),
    )(*received)
    total = pieces[0]
    for distance in range(1, reach_blocks + 1):
        total = total + shifted(pieces[distance], "sky", distance)
    return total


def solution(mesh):
    placed = (
        P(None, "sky"),
        P(("sky", "grp"), None, None),
        P(("sky", "grp"), None),
        P(("sky", "grp")),
        P(("sky", "grp")),
        P(None, None, "sky"),
        P("grp", None, None, None),
        P("grp"),
        P("grp"),
    )
    return jax.shard_map(
        on_device, mesh=mesh, in_specs=placed, out_specs=P("grp", "sky"), check_vma=False
    )
```

profile of v0, /device:TPU:1, one launch (start us, length us, event | category | flops | bytes accessed | tf_op | source)
XLA Modules:
  0.0 77.9 jit_solution(4876037405222499498)
XLA Ops:
  0.0 9.2 %collective-permute-start.2 = (f32[64,512]{1,0:T(8,128)}, f32[64,512]{1,0:T(8,128)S(1)}, u32[]{:S(2)}, u32[]{:S(2)}) collective-permute-start(f32[64,512]{1,0:T(8,128)} %s0.1), channel_id=1, source_target_pairs={{0,244},{4,248},{8,252},{12,0},{16,4},{20,8},{24,12},{28,16},{32,2... | collective-permute-start | bytes 393224 | tf_op jit(solution)/shard_map/ppermute | solution.py:17
  9.7 0.7 collective-permute-start
  10.4 1.7 %collective-permute-start.3 = (f32[64,512]{1,0:T(8,128)}, f32[64,512]{1,0:T(8,128)S(1)}, u32[]{:S(2)}, u32[]{:S(2)}) collective-permute-start(f32[64,512]{1,0:T(8,128)} %s0.1), channel_id=1, source_target_pairs={{0,240},{4,244},{8,248},{12,252},{16,0},{20,4},{24,8},{28,12},{32,... | collective-permute-start | bytes 393224 | tf_op jit(solution)/shard_map/ppermute | solution.py:17
  12.1 3.4 %copy-done.1 = bf16[128,64,512]{2,1,0:T(8,128)(2,1)S(1)} copy-done((bf16[128,64,512]{2,1,0:T(8,128)(2,1)S(1)}, bf16[128,64,512]{2,1,0:T(8,128)(2,1)}, u32[]{:S(2)}) %copy-start.1) | copy-done | bytes 8388632
  15.5 0.9 %copy-done.4 = bf16[32,3,3,128]{3,0,2,1:T(8,128)(2,1)S(1)} copy-done((bf16[32,3,3,128]{3,0,2,1:T(8,128)(2,1)S(1)}, bf16[32,3,3,128]{3,0,2,1:T(8,128)(2,1)}, u32[]{:S(2)}) %copy-start.4) | copy-done | bytes 73752
  16.4 0.7 copy-done.6
  17.7 20.2 %shard_map.91 = (f32[64,512]{1,0:T(8,128)S(1)}, f32[32,128]{1,0:T(8,128)S(1)}, f32[32,128]{1,0:T(8,128)S(1)}) custom-call(bf16[288,128]{1,0:T(8,128)(2,1)S(1)} %bitcast.6, f32[1,32]{1,0:T(1,128)S(1)} %bitcast.7, f32[1,32]{1,0:T(1,128)S(1)} %bitcast.9, bf16[128,64,512]{2,1,0:T(8,128)(2,1)S(1)} %copy-done.1), custom_call_target="tpu_custom_call" | custom-call | flops 8000000000 | bytes 9000000 | tf_op jit(solution)/shard_map/pallas_call | solution.py:114
  37.9 1.5 %collective-permute-start.4 = (f32[32,128]{1,0:T(8,128)S(1)}, f32[32,128]{1,0:T(8,128)S(1)}, u32[]{:S(2)}, u32[]{:S(2)}) collective-permute-start(f32[32,128]{1,0:T(8,128)S(1)} %get-tuple-element.19), channel_id=1, source_target_pairs={{0,252},{4,0},{8,4},{12,8},{16,12},{20,16},{24,20},{28,24},{32,28}... | collective-permute-start | bytes 49160 | tf_op jit(solution)/shard_map/ppermute | solution.py:17
  40.1 1.0 %collective-permute-done.4.right_ref = f32[32,128]{1,0:T(8,128)S(1)} collective-permute-done((f32[32,128]{1,0:T(8,128)S(1)}, f32[32,128]{1,0:T(8,128)S(1)}, u32[]{:S(2)}, u32[]{:S(2)}) %collective-permute-start.4) | collective-permute-done | bytes 16416 | tf_op jit(solution)/shard_map/ppermute | solution.py:17
  41.2 8.7 %shard_map.92 = (f32[16,2560]{1,0:T(8,128)S(1)}, f32[16,2560]{1,0:T(8,128)S(1)}, f32[16,2560]{1,0:T(8,128)S(1)}, f32[16,2560]{1,0:T(8,128)S(1)}) custom-call(s32[4]{0:T(128)S(1)} %copy-done.5, s32[1]{0:T(128)S(6)} %copy.10.counts_ref, s32[1]{0:T(128)} %bitcast.group_ref, f32[64,512]{1,0:T(8,128)S(1)} %copy-done.3, f32[64,512]{1,0:T(8,128)S(1)} %collective-permute-done.s1, ...), custom_call_target="tpu_custom_call" | custom-call | flops 4000000000 | bytes 4000000 | tf_op jit(solution)/shard_map/pallas_call | solution.py:247
  49.9 0.7 copy-done
  50.6 3.9 %collective-permute-start.6 = (f32[16,2560]{1,0:T(8,128)S(1)}, f32[16,2560]{1,0:T(8,128)S(1)}, u32[]{:S(2)}, u32[]{:S(2)}) collective-permute-start(f32[16,2560]{1,0:T(8,128)S(1)} %get-tuple-element.22), channel_id=1, source_target_pairs={{0,2},{1,3},{2,0},{3,1},{4,6},{5,7},{6,4},{7,5},{8,10},{9,11},{10,... | collective-permute-start | bytes 491528 | tf_op jit(solution)/shard_map/ppermute | solution.py:21
  54.5 1.4 %collective-permute-done.5.b = f32[16,2560]{1,0:T(8,128)S(1)} collective-permute-done((f32[16,2560]{1,0:T(8,128)S(1)}, f32[16,2560]{1,0:T(8,128)S(1)}, u32[]{:S(2)}, u32[]{:S(2)}) %collective-permute-start.5) | collective-permute-done | bytes 163872 | tf_op jit(solution)/shard_map/ppermute | solution.py:21
  56.0 4.8 %collective-permute-done.6.c = f32[16,2560]{1,0:T(8,128)S(1)} collective-permute-done((f32[16,2560]{1,0:T(8,128)S(1)}, f32[16,2560]{1,0:T(8,128)S(1)}, u32[]{:S(2)}, u32[]{:S(2)}) %collective-permute-start.6) | collective-permute-done | bytes 163872 | tf_op jit(solution)/shard_map/ppermute | solution.py:21
  60.8 2.2 %collective-permute-done.7.d = f32[16,2560]{1,0:T(8,128)S(1)} collective-permute-done((f32[16,2560]{1,0:T(8,128)S(1)}, f32[16,2560]{1,0:T(8,128)S(1)}, u32[]{:S(2)}, u32[]{:S(2)}) %collective-permute-start.7) | collective-permute-done | bytes 163872 | tf_op jit(solution)/shard_map/ppermute | solution.py:21
  63.0 0.7 copy-done.12
  63.6 1.8 %shard_map.93 = (f32[16,512]{1,0:T(8,128)}, f32[16,512]{1,0:T(8,128)}, f32[16,512]{1,0:T(8,128)}, f32[16,512]{1,0:T(8,128)}, f32[16,512]{1,0:T(8,128)}) custom-call(f32[16,2560]{1,0:T(8,128)} %copy-done, f32[16,2560]{1,0:T(8,128)} %copy-done.10, f32[16,2560]{1,0:T(8,128)} %copy-done.11, f32[16,2560]{1,0:T(8,128)} %copy-done.12), custom_call_target="tpu_custom_call" | custom-call | flops 200000 | bytes 1000000 | tf_op jit(solution)/shard_map/pallas_call | solution.py:298
  65.5 2.6 %collective-permute-start.9 = (f32[16,512]{1,0:T(8,128)}, f32[16,512]{1,0:T(8,128)S(1)}, u32[]{:S(2)}, u32[]{:S(2)}) collective-permute-start(f32[16,512]{1,0:T(8,128)} %get-tuple-element.26), channel_id=1, source_target_pairs={{0,8},{4,12},{8,16},{12,20},{16,24},{20,28},{24,32},{28,36},{32,40... | collective-permute-start | bytes 98312 | tf_op jit(solution)/shard_map/ppermute | solution.py:17
  68.0 1.4 %collective-permute-start.10 = (f32[16,512]{1,0:T(8,128)}, f32[16,512]{1,0:T(8,128)S(1)}, u32[]{:S(2)}, u32[]{:S(2)}) collective-permute-start(f32[16,512]{1,0:T(8,128)} %get-tuple-element.27), channel_id=1, source_target_pairs={{0,12},{4,16},{8,20},{12,24},{16,28},{20,32},{24,36},{28,40},{32,4... | collective-permute-start | bytes 98312 | tf_op jit(solution)/shard_map/ppermute | solution.py:17
  69.4 1.0 %collective-permute-start.11 = (f32[16,512]{1,0:T(8,128)}, f32[16,512]{1,0:T(8,128)S(1)}, u32[]{:S(2)}, u32[]{:S(2)}) collective-permute-start(f32[16,512]{1,0:T(8,128)} %get-tuple-element.28), channel_id=1, source_target_pairs={{0,16},{4,20},{8,24},{12,28},{16,32},{20,36},{24,40},{28,44},{32,4... | collective-permute-start | bytes 98312 | tf_op jit(solution)/shard_map/ppermute | solution.py:17
  70.4 1.4 %collective-permute-done.9 = f32[16,512]{1,0:T(8,128)S(1)} collective-permute-done((f32[16,512]{1,0:T(8,128)}, f32[16,512]{1,0:T(8,128)S(1)}, u32[]{:S(2)}, u32[]{:S(2)}) %collective-permute-start.9) | collective-permute-done | bytes 32800 | tf_op jit(solution)/shard_map/ppermute | solution.py:17
  71.8 3.1 %collective-permute-done.10 = f32[16,512]{1,0:T(8,128)S(1)} collective-permute-done((f32[16,512]{1,0:T(8,128)}, f32[16,512]{1,0:T(8,128)S(1)}, u32[]{:S(2)}, u32[]{:S(2)}) %collective-permute-start.10) | collective-permute-done | bytes 32800 | tf_op jit(solution)/shard_map/ppermute | solution.py:17
  74.9 1.6 %collective-permute-done.11 = f32[16,512]{1,0:T(8,128)S(1)} collective-permute-done((f32[16,512]{1,0:T(8,128)}, f32[16,512]{1,0:T(8,128)S(1)}, u32[]{:S(2)}, u32[]{:S(2)}) %collective-permute-start.11) | collective-permute-done | bytes 32800 | tf_op jit(solution)/shard_map/ppermute | solution.py:17
  76.5 1.4 %add_add_fusion = f32[16,512]{1,0:T(8,128)} fusion(f32[16,512]{1,0:T(8,128)S(1)} %collective-permute-done.11, f32[16,512]{1,0:T(8,128)S(1)} %collective-permute-done.10, f32[16,512]{1,0:T(8,128)S(1)} %collective-permute-done.9, f32[16,512]{1,0:T(8,128)} %get-tuple-element.24, f32[16,512]{1,0:T(8,128)S(1)} %collective-permute-done.8), kind=kLoop, calls=%fused_computation | loop fusion | flops 32768 | bytes 196608 | tf_op jit(solution)/shard_map/add | solution.py:305
  (33 shorter events, 1.3 us)
Async XLA Ops:
  0.0 41.2 %collective-permute-start.2 = (f32[64,512]{1,0:T(8,128)}, f32[64,512]{1,0:T(8,128)S(1)}, u32[]{:S(2)}, u32[]{:S(2)}) collective-permute-start(f32[64,512]{1,0:T(8,128)} %s0.1), channel_id=1, source_target_pairs={{0,244},{4,248},{8,252},{12,0},{16,4},{20,8},{24,12},{28,16},{32,2... | collective-permute-start | bytes 393224 | tf_op jit(solution)/shard_map/ppermute | solution.py:17
  9.2 32.0 %collective-permute-start.1 = (f32[64,512]{1,0:T(8,128)}, f32[64,512]{1,0:T(8,128)S(1)}, u32[]{:S(2)}, u32[]{:S(2)}) collective-permute-start(f32[64,512]{1,0:T(8,128)} %s0.1), channel_id=1, source_target_pairs={{0,248},{4,252},{8,0},{12,4},{16,8},{20,12},{24,16},{28,20},{32,24... | collective-permute-start | bytes 393224 | tf_op jit(solution)/shard_map/ppermute | solution.py:17
  9.7 31.5 %collective-permute-start = (f32[64,512]{1,0:T(8,128)}, f32[64,512]{1,0:T(8,128)S(1)}, u32[]{:S(2)}, u32[]{:S(2)}) collective-permute-start(f32[64,512]{1,0:T(8,128)} %s0.1), channel_id=1, source_target_pairs={{0,252},{4,0},{8,4},{12,8},{16,12},{20,16},{24,20},{28,24},{32,28}... | collective-permute-start | bytes 393224 | tf_op jit(solution)/shard_map/ppermute | solution.py:17
  10.4 30.8 %collective-permute-start.3 = (f32[64,512]{1,0:T(8,128)}, f32[64,512]{1,0:T(8,128)S(1)}, u32[]{:S(2)}, u32[]{:S(2)}) collective-permute-start(f32[64,512]{1,0:T(8,128)} %s0.1), channel_id=1, source_target_pairs={{0,240},{4,244},{8,248},{12,252},{16,0},{20,4},{24,8},{28,12},{32,... | collective-permute-start | bytes 393224 | tf_op jit(solution)/shard_map/ppermute | solution.py:17
  12.1 3.4 %copy-start.1 = (bf16[128,64,512]{2,1,0:T(8,128)(2,1)S(1)}, bf16[128,64,512]{2,1,0:T(8,128)(2,1)}, u32[]{:S(2)}) copy-start(bf16[128,64,512]{2,1,0:T(8,128)(2,1)} %x_ref.1) | copy-start | bytes 25165828
  15.5 0.9 %copy-start.4 = (bf16[32,3,3,128]{3,0,2,1:T(8,128)(2,1)S(1)}, bf16[32,3,3,128]{3,0,2,1:T(8,128)(2,1)}, u32[]{:S(2)}) copy-start(bf16[32,3,3,128]{3,0,2,1:T(8,128)(2,1)} %param.15) | copy-start | bytes 221188
  17.7 22.5 %copy-start.13 = (f32[4,256]{1,0:T(4,128)S(1)}, f32[4,256]{1,0:T(4,128)}, u32[]{:S(2)}) copy-start(f32[4,256]{1,0:T(4,128)} %param.11) | copy-start | bytes 12292
  17.7 23.5 %copy-start.2 = (f32[4,64,2048]{2,1,0:T(8,128)S(1)}, f32[4,64,2048]{2,1,0:T(8,128)}, u32[]{:S(2)}) copy-start(f32[4,64,2048]{2,1,0:T(8,128)} %record_ref.1) | copy-start | bytes 6291460
  17.7 23.5 %copy-start.3 = (f32[64,512]{1,0:T(8,128)S(1)}, f32[64,512]{1,0:T(8,128)}, u32[]{:S(2)}) copy-start(f32[64,512]{1,0:T(8,128)} %s0.1) | copy-start | bytes 393220
  17.7 23.6 %copy-start.5 = (s32[4]{0:T(128)S(1)}, s32[4]{0:T(128)}, u32[]{:S(2)}) copy-start(s32[4]{0:T(128)} %offsets_ref.1) | copy-start | bytes 52
  17.7 23.6 %copy-start.7 = (f32[32]{0:T(128)S(1)}, f32[32]{0:T(128)}, u32[]{:S(2)}) copy-start(f32[32]{0:T(128)} %param.16) | copy-start | bytes 388
  17.7 23.6 %copy-start.9 = (f32[32]{0:T(128)S(1)}, f32[32]{0:T(128)}, u32[]{:S(2)}) copy-start(f32[32]{0:T(128)} %param.17) | copy-start | bytes 388
  37.9 3.2 %collective-permute-start.4 = (f32[32,128]{1,0:T(8,128)S(1)}, f32[32,128]{1,0:T(8,128)S(1)}, u32[]{:S(2)}, u32[]{:S(2)}) collective-permute-start(f32[32,128]{1,0:T(8,128)S(1)} %get-tuple-element.19), channel_id=1, source_target_pairs={{0,252},{4,0},{8,4},{12,8},{16,12},{20,16},{24,20},{28,24},{32,28}... | collective-permute-start | bytes 49160 | tf_op jit(solution)/shard_map/ppermute | solution.py:17
  49.9 0.7 copy-start
  50.6 5.4 %collective-permute-start.5 = (f32[16,2560]{1,0:T(8,128)S(1)}, f32[16,2560]{1,0:T(8,128)S(1)}, u32[]{:S(2)}, u32[]{:S(2)}) collective-permute-start(f32[16,2560]{1,0:T(8,128)S(1)} %get-tuple-element.21), channel_id=1, source_target_pairs={{0,1},{1,0},{2,3},{3,2},{4,5},{5,4},{6,7},{7,6},{8,9},{9,8},{10,11... | collective-permute-start | bytes 491528 | tf_op jit(solution)/shard_map/ppermute | solution.py:21
  50.6 10.2 %collective-permute-start.6 = (f32[16,2560]{1,0:T(8,128)S(1)}, f32[16,2560]{1,0:T(8,128)S(1)}, u32[]{:S(2)}, u32[]{:S(2)}) collective-permute-start(f32[16,2560]{1,0:T(8,128)S(1)} %get-tuple-element.22), channel_id=1, source_target_pairs={{0,2},{1,3},{2,0},{3,1},{4,6},{5,7},{6,4},{7,5},{8,10},{9,11},{10,... | collective-permute-start | bytes 491528 | tf_op jit(solution)/shard_map/ppermute | solution.py:21
  54.5 8.4 %collective-permute-start.7 = (f32[16,2560]{1,0:T(8,128)S(1)}, f32[16,2560]{1,0:T(8,128)S(1)}, u32[]{:S(2)}, u32[]{:S(2)}) collective-permute-start(f32[16,2560]{1,0:T(8,128)S(1)} %get-tuple-element.23), channel_id=1, source_target_pairs={{0,3},{1,2},{2,1},{3,0},{4,7},{5,6},{6,5},{7,4},{8,11},{9,10},{10,... | collective-permute-start | bytes 491528 | tf_op jit(solution)/shard_map/ppermute | solution.py:21
  56.0 7.0 %copy-start.10 = (f32[16,2560]{1,0:T(8,128)}, f32[16,2560]{1,0:T(8,128)S(1)}, u32[]{:S(2)}) copy-start(f32[16,2560]{1,0:T(8,128)S(1)} %collective-permute-done.5.b) | copy-start | bytes 491524
  60.8 2.2 %copy-start.11 = (f32[16,2560]{1,0:T(8,128)}, f32[16,2560]{1,0:T(8,128)S(1)}, u32[]{:S(2)}) copy-start(f32[16,2560]{1,0:T(8,128)S(1)} %collective-permute-done.6.c) | copy-start | bytes 491524
  63.0 0.7 copy-start.12
  65.5 5.0 %collective-permute-start.8 = (f32[16,512]{1,0:T(8,128)}, f32[16,512]{1,0:T(8,128)S(1)}, u32[]{:S(2)}, u32[]{:S(2)}) collective-permute-start(f32[16,512]{1,0:T(8,128)} %get-tuple-element.25), channel_id=1, source_target_pairs={{0,4},{4,8},{8,12},{12,16},{16,20},{20,24},{24,28},{28,32},{32,36}... | collective-permute-start | bytes 98312 | tf_op jit(solution)/shard_map/ppermute | solution.py:17
  65.5 6.4 %collective-permute-start.9 = (f32[16,512]{1,0:T(8,128)}, f32[16,512]{1,0:T(8,128)S(1)}, u32[]{:S(2)}, u32[]{:S(2)}) collective-permute-start(f32[16,512]{1,0:T(8,128)} %get-tuple-element.26), channel_id=1, source_target_pairs={{0,8},{4,12},{8,16},{12,20},{16,24},{20,28},{24,32},{28,36},{32,40... | collective-permute-start | bytes 98312 | tf_op jit(solution)/shard_map/ppermute | solution.py:17
  68.0 6.9 %collective-permute-start.10 = (f32[16,512]{1,0:T(8,128)}, f32[16,512]{1,0:T(8,128)S(1)}, u32[]{:S(2)}, u32[]{:S(2)}) collective-permute-start(f32[16,512]{1,0:T(8,128)} %get-tuple-element.27), channel_id=1, source_target_pairs={{0,12},{4,16},{8,20},{12,24},{16,28},{20,32},{24,36},{28,40},{32,4... | collective-permute-start | bytes 98312 | tf_op jit(solution)/shard_map/ppermute | solution.py:17
  69.4 7.1 %collective-permute-start.11 = (f32[16,512]{1,0:T(8,128)}, f32[16,512]{1,0:T(8,128)S(1)}, u32[]{:S(2)}, u32[]{:S(2)}) collective-permute-start(f32[16,512]{1,0:T(8,128)} %get-tuple-element.28), channel_id=1, source_target_pairs={{0,16},{4,20},{8,24},{12,28},{16,32},{20,36},{24,40},{28,44},{32,4... | collective-permute-start | bytes 98312 | tf_op jit(solution)/shard_map/ppermute | solution.py:17
  (2 other events, 1.3 us)
where the time goes:
time: 78 us; the launch traced here: 77.9 us
  Pallas kernels  30.7 us (39%)
  starting transfers between devices  22.5 us (29%)
  waiting for transfers between devices  15.6 us (20%)
  local copies, waits for them, and re-layouts  6.93 us (9%)
  other arithmetic  1.39 us (2%)
  between operations  0.78 us (1%)
    pallas_call x1, Pallas kernels, conv_prior(): pl.pallas_call(conv_kernel, grid=(strip_rows // rows,), in_specs=[full((9...  20.2 us
    ppermute x9, starting transfers between devices, shifted(): lax.ppermute(x, axis, [(i, (i + by) % length) for i in range(length)])  18.6 us
    pallas_call x1, Pallas kernels, exposure_terms(): pl.pallas_call(exposure_kernel, grid_spec=pltpu.PrefetchScalarGridSpec(nu...  8.68 us
    ppermute x3, waiting for transfers between devices, partner(): lax.ppermute(x, axis, [(i, i ^ mask) for i in range(lax.axis_size(axis))])  8.44 us
    ppermute x9, waiting for transfers between devices, shifted(): lax.ppermute(x, axis, [(i, (i + by) % length) for i in range(length)])  7.16 us
    unnamed x28, local copies, waits for them, and re-layouts  6.93 us
    ppermute x3, starting transfers between devices, partner(): lax.ppermute(x, axis, [(i, i ^ mask) for i in range(lax.axis_size(axis))])  3.92 us
    pallas_call x1, Pallas kernels, on_device(): pl.pallas_call(sum_kernel, out_shape=[jax.ShapeDtypeStruct((share, cols),...  1.82 us
  transfers between devices with their start and end apart: 12, of which 7 were waited for; matrix products, arithmetic and copies ran while one was open for 0% of the time, Pallas kernels for 26%

commit v1 on v0

--- a/solution.py
+++ b/solution.py
@@ -36,104 +36,140 @@
     return hidden * (1.0 + jnp.tanh(0.5 * hidden)) * half_weight
 
 
-def conv_kernel(w_ref, bias_ref, ow_ref, x_ref, prior_ref, left_ref, right_ref, t_ref, p_ref, carry_ref):
+def conv_kernel(w_ref, bias_ref, ow_ref, *refs):
+    x_refs, (prior_ref, left_ref, right_ref, t_ref, a_ref, b_ref) = refs[:-6], refs[-6:]
     step = pl.program_id(0)
-    channels, rows, cols = x_ref.shape
+    channels = w_ref.shape[1]
+    cols = prior_ref.shape[1]
     outs = bias_ref.shape[1]
     taps = 3 * outs
-    depth = channels * rows
+    block = 8
+    pairs = block // 2
 
     @pl.when(step == 0)
     def _():
-        repeat = jnp.where(
-            lane_index((channels, depth)) // rows == lax.broadcasted_iota(jnp.int32, (channels, depth), 0), 1.0, 0.0
-        ).astype(BF16)
-        spread = jnp.dot(w_ref[...], repeat, preferred_element_type=F32)
-        row_in = lane_index((taps, depth)) % rows
-        for j in range(rows + 2):
-            band = jnp.zeros((taps, depth), F32)
-            for a in range(3):
-                band = jnp.where(row_in == j - 2 + a, spread[a * taps : (a + 1) * taps], band)
-            t_ref[j * taps : (j + 1) * taps, :] = band.astype(BF16)
-        carry_ref[...] = jnp.zeros_like(carry_ref)
+        w = [w_ref[a * taps : (a + 1) * taps, :] for a in range(3)]
+        none = jnp.zeros_like(w[0])
+        for j, (even, odd) in enumerate(((w[2], none), (w[1], w[2]), (w[0], w[1]), (none, w[0]))):
+            t_ref[j * taps : (j + 1) * taps, :channels] = even
+            t_ref[j * taps : (j + 1) * taps, channels:] = odd
+        b_ref[pairs - 1] = jnp.zeros(b_ref.shape[1:], F32)
         left_ref[...] = jnp.zeros_like(left_ref)
         right_ref[...] = jnp.zeros_like(right_ref)
 
-    @pl.when(step > 0)
-    def _():
-        carry_ref[...] = p_ref[rows * taps :, :]
-
-    x = x_ref[...].reshape(depth, cols)
-    p_ref[...] = jnp.dot(t_ref[...], x, preferred_element_type=F32)
-
     bias = column(bias_ref[...])
     half_weight = column(ow_ref[...]) * 0.5
-    lane = lane_index((1, LANES))
+    lane = lane_index((outs, LANES))
     col = lane_index((1, cols))
     inner = jnp.logical_and(col > 0, col < cols - 1)
 
-    def one_row(i, carried):
-        row = step * rows - 1 + i
-        parts = []
-        for b in range(3):
-            part = p_ref[i * taps + b * outs : i * taps + (b + 1) * outs, :]
-            if carried:
-                part = part + carry_ref[i * taps + b * outs : i * taps + (b + 1) * outs, :]
-            parts.append(part)
-        before, here, after = parts
+    def load(half):
+        parts = [jnp.swapaxes(x[:, half * block : (half + 1) * block, :], 0, 1) for x in x_refs]
+        return jnp.concatenate(parts, axis=1)
+
+    def multiply(p_ref, x, pair):
+        both = x[2 * pair : 2 * pair + 2].reshape(2 * channels, cols)
+        p_ref[pair] = jnp.dot(t_ref[...], both, preferred_element_type=F32)
+
+    def finish(first, terms, base, r, edges):
+        (p1, n1, j1), (p2, n2, j2) = terms
+        before, here, after = [
+            p1[n1, j1 * taps + b * outs : j1 * taps + (b + 1) * outs, :]
+            + p2[n2, j2 * taps + b * outs : j2 * taps + (b + 1) * outs, :]
+            for b in range(3)
+        ]
+        last_row(before, here, after, base, r, edges)
+
+    def last_row(before, here, after, base, r, edges):
         hidden = pltpu.roll(before, 1, 1) + here + pltpu.roll(after, cols - 1, 1) + bias
         score = jnp.sum(weighted_silu(hidden, half_weight), axis=0, keepdims=True)
-        prior_ref[pl.ds(row, 1), :] = jnp.where(inner, score, 0.0)
-        mine = (lane >> 1) == row
+        prior_ref[pl.ds(base + block + r, 1), :] = jnp.where(inner, score, 0.0)
+        mine = (lane >> 1) == r + 1
         tail = before[:, cols - LANES :] + jnp.where(
             lane == LANES - 2, pltpu.roll(here[:, cols - LANES :], LANES - 1, 1), 0.0
         )
-        left_ref[...] += jnp.where(mine, pltpu.roll(tail, 2 * row + 2, 1), 0.0)
         head = after[:, :LANES] + jnp.where(lane == 1, pltpu.roll(here[:, :LANES], 1, 1), 0.0)
-        right_ref[...] += jnp.where(mine, pltpu.roll(head, 2 * row, 1), 0.0)
-
-    @pl.when(step > 0)
-    def _():
-        one_row(0, True)
-
-    for i in range(1, rows):
-        one_row(i, i < 2)
+        edges[0] = jnp.where(mine, pltpu.roll(tail, (2 * r + 4) % LANES, 1), edges[0])
+        edges[1] = jnp.where(mine, pltpu.roll(head, (2 * r + 2) % LANES, 1), edges[1])
+
+    def no_edges():
+        return [jnp.zeros((outs, LANES), F32), jnp.zeros((outs, LANES), F32)]
+
+    def keep_edges(edges, base):
+        valid = base - 1 + (lane >> 1) >= 0
+        turn = (2 * base + LANES - 2) % LANES
+        left_ref[...] += pltpu.roll(jnp.where(valid, edges[0], 0.0), turn, 1)
+        right_ref[...] += pltpu.roll(jnp.where(valid, edges[1], 0.0), turn, 1)
+
+    def inner_rows(p_ref, base, edges, pair):
+        for r in (2 * pair + 1, 2 * pair + 2):
+            finish(None, ((p_ref, pair, r - 2 * pair + 1), (p_ref, pair + 1, r - 2 * pair - 1)), base, r, edges)
+
+    def first_rows(p_ref, earlier_ref, base, edges):
+        for r in (-1, 0):
+            finish(None, ((earlier_ref, pairs - 1, r + 3), (p_ref, 0, r + 1)), base, r, edges)
+
+    def phase(p_ref, earlier_ref, half, base):
+        x = load(half)
+        edges = no_edges()
+        for pair in range(pairs):
+            multiply(p_ref, x, pair)
+            if pair < pairs - 1:
+                inner_rows(earlier_ref, base - block, edges, pair)
+        keep_edges(edges, base - block)
+        edges = no_edges()
+        first_rows(p_ref, earlier_ref, base, edges)
+        keep_edges(edges, base)
+
+    start = step * 2 * block
+    phase(a_ref, b_ref, 0, start)
+    phase(b_ref, a_ref, 1, start + block)
 
     @pl.when(step == pl.num_programs(0) - 1)
     def _():
-        one_row(rows, False)
+        edges = no_edges()
+        base = start + block
+        for pair in range(pairs - 1):
+            inner_rows(b_ref, base, edges, pair)
+        r = block - 1
+        j = r - 2 * (pairs - 1) + 1
+        before, here, after = [
+            b_ref[pairs - 1, j * taps + b * outs : j * taps + (b + 1) * outs, :] for b in range(3)
+        ]
+        last_row(before, here, after, base, r, edges)
+        keep_edges(edges, base)
 
 
 def conv_prior(features, weight, bias, out_weight):
     channels, strip_rows, cols = features.shape
     outs = bias.shape[0]
-    rows = 8
+    block = 8
     taps = 3 * outs
+    cuts = 4
     flat = weight.transpose(1, 2, 0, 3).reshape(9 * outs, channels)
     full = lambda shape: pl.BlockSpec(shape, lambda i: (0,) * len(shape))
     return pl.pallas_call(
         conv_kernel,
-        grid=(strip_rows // rows,),
-        in_specs=[
-            full((9 * outs, channels)),
-            full((1, outs)),
-            full((1, outs)),
-            pl.BlockSpec((channels, rows, cols), lambda i: (0, i, 0)),
+        grid=(strip_rows // (2 * block),),
+        in_specs=[full((9 * outs, channels)), full((1, outs)), full((1, outs))]
+        + [
+            pl.BlockSpec((channels // cuts, 2 * block, cols), functools.partial(lambda n, i: (n, i, 0), n))
+            for n in range(cuts)
         ],
-        out_specs=[full((strip_rows, cols)), full((outs, LANES)), full((outs, LANES))],
+        out_specs=[full((strip_rows + block, cols)), full((outs, LANES)), full((outs, LANES))],
         out_shape=[
-            jax.ShapeDtypeStruct((strip_rows, cols), F32),
+            jax.ShapeDtypeStruct((strip_rows + block, cols), F32),
             jax.ShapeDtypeStruct((outs, LANES), F32),
             jax.ShapeDtypeStruct((outs, LANES), F32),
         ],
         scratch_shapes=[
-            pltpu.VMEM(((rows + 2) * taps, channels * rows), BF16),
-            pltpu.VMEM(((rows + 2) * taps, cols), F32),
-            pltpu.VMEM((2 * taps, cols), F32),
+            pltpu.VMEM((4 * taps, 2 * channels), BF16),
+            pltpu.VMEM((block // 2, 4 * taps, cols), F32),
+            pltpu.VMEM((block // 2, 4 * taps, cols), F32),
         ],
-        compiler_params=pltpu.CompilerParams(vmem_limit_bytes=40 << 20),
+        compiler_params=pltpu.CompilerParams(vmem_limit_bytes=60 << 20),
         cost_estimate=pl.CostEstimate(flops=8_000_000_000, bytes_accessed=9_000_000, transcendentals=1_000_000),
-    )(flat, bias.reshape(1, outs), out_weight.reshape(1, outs), features)
+    )(flat, bias.reshape(1, outs), out_weight.reshape(1, outs), *([features] * cuts))
 
 
 def split(x):
@@ -142,8 +178,8 @@
 
 
 def exposure_kernel(
-    offsets_ref, counts_ref, group_ref, s0, s1, s2, s3, s4, record_ref, taps_ref, prior_ref, left_ref, right_ref,
-    bias_ref, ow_ref, o0, o1, o2, o3, ext_ref, acc_ref,
+    offsets_ref, counts_ref, s0, s1, s2, s3, s4, record_ref, taps_ref, prior_ref, left_ref, right_ref,
+    bias_ref, ow_ref, keep_ref, give_ref, ext_ref, acc_ref,
 ):
     slot = pl.program_id(0)
     rows, cols = s0.shape
@@ -157,7 +193,7 @@
         for d, part in enumerate((s0, s1, s2, s3, s4)):
             ext_ref[:, d * cols : (d + 1) * cols] = part[...]
         acc_ref[:, cols:] = jnp.zeros((rows, acc_ref.shape[1] - cols), F32)
-        acc_ref[:, :cols] = prior_ref[...]
+        acc_ref[:, :cols] = prior_ref[prior_ref.shape[0] - rows :, :]
         edge = left_ref[...] + right_ref[...] + column(bias_ref[...])
         score = jnp.sum(weighted_silu(edge, column(ow_ref[...]) * 0.5), axis=0, keepdims=True)
         lane = lane_index((rows, LANES))
@@ -231,79 +267,99 @@
 
     @pl.when(slot == pl.num_programs(0) - 1)
     def _():
-        share = o0.shape[0]
-        for k, out in enumerate((o0, o1, o2, o3)):
-            first = pl.multiple_of((group_ref[0] ^ k) * share, share)
-            out[...] = acc_ref[pl.ds(first, share), :]
-
-
-def exposure_terms(group, offsets, counts, sky_parts, exposures, psf_taps, prior, left, right, bias, out_weight, n_grp):
+        for d in range(5):
+            to_ref = give_ref if d % 2 else keep_ref
+            to_ref[:, d // 2 * cols : (d // 2 + 1) * cols] = acc_ref[:, d * cols : (d + 1) * cols]
+
+
+def exposure_terms(offsets, counts, sky_parts, exposures, psf_taps, prior, left, right, bias, out_weight):
     slots, rows, width = exposures.shape
     cols = sky_parts[0].shape[1]
     reach = len(sky_parts) * cols
     outs = bias.shape[0]
-    share = rows // n_grp
     full = lambda shape: pl.BlockSpec(shape, lambda i, *_: (0,) * len(shape))
     return pl.pallas_call(
         exposure_kernel,
         grid_spec=pltpu.PrefetchScalarGridSpec(
-            num_scalar_prefetch=3,
+            num_scalar_prefetch=2,
             grid=(slots,),
             in_specs=[full((rows, cols))] * len(sky_parts)
             + [
                 pl.BlockSpec((1, rows, width), lambda i, *_: (i, 0, 0)),
                 pl.BlockSpec((1, 1, psf_taps.shape[1]), lambda i, *_: (i, 0, 0)),
-                full((rows, cols)),
+                full(prior.shape),
                 full((outs, LANES)),
                 full((outs, LANES)),
                 full((1, outs)),
                 full((1, outs)),
             ],
-            out_specs=[full((share, reach))] * n_grp,
+            out_specs=[full((rows, 3 * cols)), full((rows, 2 * cols))],
             scratch_shapes=[pltpu.VMEM((rows, reach), F32), pltpu.VMEM((rows, reach), F32)],
         ),
-        out_shape=[jax.ShapeDtypeStruct((share, reach), F32)] * n_grp,
+        out_shape=[jax.ShapeDtypeStruct((rows, 3 * cols), F32), jax.ShapeDtypeStruct((rows, 2 * cols), F32)],
         compiler_params=pltpu.CompilerParams(vmem_limit_bytes=40 << 20),
         cost_estimate=pl.CostEstimate(flops=4_000_000_000, bytes_accessed=4_000_000, transcendentals=0),
     )(
-        offsets, counts, group, *sky_parts, exposures, psf_taps.reshape(slots, 1, -1), prior, left, right,
+        offsets, counts, *sky_parts, exposures, psf_taps.reshape(slots, 1, -1), prior, left, right,
         bias.reshape(1, outs), out_weight.reshape(1, outs),
     )
 
 
+def join_kernel(keep_ref, got_ref, *outs):
+    second = lax.axis_index("sky") % 2 == 1
+    group = lax.axis_index("grp")
+    share, width = outs[0].shape
+    cols = width // 3
+    for k, out in enumerate(outs):
+        first = pl.multiple_of((group ^ k) * share, share)
+        low = got_ref[pl.ds(first, share), :cols]
+        high = got_ref[pl.ds(first, share), cols:]
+        for d, extra in enumerate(
+            (jnp.where(second, low, 0.0), jnp.where(second, high, low), jnp.where(second, 0.0, high))
+        ):
+            cut = slice(d * cols, (d + 1) * cols)
+            out[:, cut] = keep_ref[pl.ds(first, share), cut] + extra
+
+
 def sum_kernel(a, b, c, d, *outs):
-    total = a[...] + b[...] + c[...] + d[...]
     cols = outs[0].shape[1]
     for k, out in enumerate(outs):
-        out[...] = total[:, k * cols : (k + 1) * cols]
+        cut = slice(k * cols, (k + 1) * cols)
+        out[...] = (a[:, cut] + b[:, cut]) + (c[:, cut] + d[:, cut])
+
+
+def small_call(kernel, out_shapes, *operands):
+    near = pl.BlockSpec(memory_space=pltpu.VMEM)
+    return pl.pallas_call(
+        kernel,
+        in_specs=[near] * len(operands),
+        out_specs=[near] * len(out_shapes),
+        out_shape=[jax.ShapeDtypeStruct(shape, F32) for shape in out_shapes],
+        compiler_params=pltpu.CompilerParams(vmem_limit_bytes=8 << 20),
+        cost_estimate=pl.CostEstimate(flops=200_000, bytes_accessed=1_000_000, transcendentals=0),
+    )(*operands)
 
 
 def on_device(
     sky_strip, exposures, psf_taps, offsets, counts, features, conv_weight, conv_bias, out_weight
 ):
     n_grp = lax.axis_size("grp")
-    cols = sky_strip.shape[1]
+    strip_rows, cols = sky_strip.shape
+    share = strip_rows // n_grp
     reach_blocks = exposures.shape[2] // cols
     parts = [sky_strip]
     for distance in range(1, reach_blocks + 1):
         parts.append(shifted(sky_strip, "sky", -distance))
     prior, left, right = conv_prior(features, conv_weight, conv_bias, out_weight)
     right = shifted(right, "sky", -1)
-    group = lax.axis_index("grp").astype(jnp.int32).reshape(1)
-    terms = exposure_terms(
-        group, offsets, counts, parts, exposures, psf_taps, prior, left, right, conv_bias, out_weight, n_grp
+    keep, give = exposure_terms(
+        offsets, counts, parts, exposures, psf_taps, prior, left, right, conv_bias, out_weight
     )
+    got = partner(give, "sky", 1)
+    terms = small_call(join_kernel, [(share, 3 * cols)] * n_grp, keep, got)
     received = [terms[0]] + [partner(terms[k], "grp", k) for k in range(1, n_grp)]
-    share = terms[0].shape[0]
-    pieces = pl.pallas_call(
-        sum_kernel,
-        out_shape=[jax.ShapeDtypeStruct((share, cols), F32)] * (reach_blocks + 1),
-        cost_estimate=pl.CostEstimate(flops=200_000, bytes_accessed=1_000_000, transcendentals=0),
-    )(*received)
-    total = pieces[0]
-    for distance in range(1, reach_blocks + 1):
-        total = total + shifted(pieces[distance], "sky", distance)
-    return total
+    own, near, far = small_call(sum_kernel, [(share, cols)] * 3, *received)
+    return own + shifted(near, "sky", 2) + shifted(far, "sky", 4)
 
 
 def solution(mesh):

time: 78 us -> 58.8 us (0.75)
  Pallas kernels: 30.7 us -> 15.8 us
  local copies, waits for them, and re-layouts: 6.93 us -> 1.65 us
  starting transfers between devices: 22.5 us -> 27.6 us
  waiting for transfers between devices: 15.6 us -> 12.7 us
    pallas_call x2 -> x3, Pallas kernels: 22.1 us -> 12.9 us  [the longest x1 12.9 us: conv_prior(): pl.pallas_call(conv_kernel, grid=(strip_rows // (2 * block),), in_specs=[...]
    ppermute x3 -> x4, starting transfers between devices: 3.92 us -> 10.3 us  [partner(): lax.ppermute(x, axis, [(i, i ^ mask) for i in range(lax.axis_size(axis))])]
    pallas_call x1, Pallas kernels: 8.68 us -> 2.84 us  [exposure_terms(): pl.pallas_call(exposure_kernel, grid_spec=pltpu.PrefetchScalarGridSpec(nu...]
    unnamed x28 -> x16, local copies, waits for them, and re-layouts: 6.93 us -> 1.64 us
    ppermute x9 -> x7, waiting for transfers between devices: 7.16 us -> 4.06 us  [shifted(): lax.ppermute(x, axis, [(i, (i + by) % length) for i in range(length)])]
    ppermute x9 -> x7, starting transfers between devices: 18.6 us -> 17.3 us  [shifted(): lax.ppermute(x, axis, [(i, (i + by) % length) for i in range(length)])]
    ppermute x3 -> x4, waiting for transfers between devices: 8.44 us -> 8.62 us  [partner(): lax.ppermute(x, axis, [(i, i ^ mask) for i in range(lax.axis_size(axis))])]
  transfers between devices with their start and end apart: 12 -> 11, of which waited for: 7 -> 7; matrix products, arithmetic and copies ran while one was open for 0% -> 0% of each run, Pallas kernels for 26% -> 22%
where the time goes in v1:
time: 58.8 us; the launch traced here: 59.1 us
  starting transfers between devices  27.6 us (47%)
  Pallas kernels  15.8 us (27%)
  waiting for transfers between devices  12.7 us (22%)
  local copies, waits for them, and re-layouts  1.65 us (3%)
  between operations  0.79 us (1%)
  other arithmetic  0.62 us (1%)
    ppermute x7, starting transfers between devices, shifted(): lax.ppermute(x, axis, [(i, (i + by) % length) for i in range(length)])  17.3 us
    pallas_call x1, Pallas kernels, conv_prior(): pl.pallas_call(conv_kernel, grid=(strip_rows // (2 * block),), in_specs=[...  12.9 us
    ppermute x4, starting transfers between devices, partner(): lax.ppermute(x, axis, [(i, i ^ mask) for i in range(lax.axis_size(axis))])  10.3 us
    ppermute x4, waiting for transfers between devices, partner(): lax.ppermute(x, axis, [(i, i ^ mask) for i in range(lax.axis_size(axis))])  8.62 us
    ppermute x7, waiting for transfers between devices, shifted(): lax.ppermute(x, axis, [(i, (i + by) % length) for i in range(length)])  4.06 us
    pallas_call x1, Pallas kernels, exposure_terms(): pl.pallas_call(exposure_kernel, grid_spec=pltpu.PrefetchScalarGridSpec(nu...  2.84 us
    unnamed x16, local copies, waits for them, and re-layouts  1.64 us
  transfers between devices with their start and end apart: 11, of which 7 were waited for; matrix products, arithmetic and copies ran while one was open for 0% of the time, Pallas kernels for 22%

profile of v1, /device:TPU:1, one launch (start us, length us, event | category | flops | bytes accessed | tf_op | source)
XLA Modules:
  0.0 59.1 jit_solution(11152949065007149066)
XLA Ops:
  0.0 9.2 %collective-permute-start.2 = (f32[64,512]{1,0:T(8,128)}, f32[64,512]{1,0:T(8,128)S(1)}, u32[]{:S(2)}, u32[]{:S(2)}) collective-permute-start(f32[64,512]{1,0:T(8,128)} %s0.1), channel_id=1, source_target_pairs={{0,244},{4,248},{8,252},{12,0},{16,4},{20,8},{24,12},{28,16},{32,2... | collective-permute-start | bytes 393224 | tf_op jit(solution)/shard_map/ppermute | solution.py:17
  9.2 0.5 collective-permute-start.1
  9.7 0.7 %collective-permute-start = (f32[64,512]{1,0:T(8,128)}, f32[64,512]{1,0:T(8,128)S(1)}, u32[]{:S(2)}, u32[]{:S(2)}) collective-permute-start(f32[64,512]{1,0:T(8,128)} %s0.1), channel_id=1, source_target_pairs={{0,252},{4,0},{8,4},{12,8},{16,12},{20,16},{24,20},{28,24},{32,28}... | collective-permute-start | bytes 393224 | tf_op jit(solution)/shard_map/ppermute | solution.py:17
  10.4 1.7 %collective-permute-start.3 = (f32[64,512]{1,0:T(8,128)}, f32[64,512]{1,0:T(8,128)S(1)}, u32[]{:S(2)}, u32[]{:S(2)}) collective-permute-start(f32[64,512]{1,0:T(8,128)} %s0.1), channel_id=1, source_target_pairs={{0,240},{4,244},{8,248},{12,252},{16,0},{20,4},{24,8},{28,12},{32,... | collective-permute-start | bytes 393224 | tf_op jit(solution)/shard_map/ppermute | solution.py:17
  12.1 12.9 %shard_map.91 = (f32[72,512]{1,0:T(8,128)}, f32[32,128]{1,0:T(8,128)}, f32[32,128]{1,0:T(8,128)}) custom-call(bf16[288,128]{1,0:T(8,128)(2,1)} %bitcast.9, f32[1,32]{1,0:T(1,128)} %bitcast.5, f32[1,32]{1,0:T(1,128)} %bitcast.7, bf16[128,64,512]{2,1,0:T(8,128)(2,1)} %refs_3_.1, bf16[128,64,512]{2,1,0:T(8,128)(2,1)} %refs_3_.1, bf16[128,64,512]{2,1,0:T(8,128)(2,1)} %refs_3_.1, ...), custom_call_target="tpu_custom_call" | custom-call | flops 8000000000 | bytes 9000000 | tf_op jit(solution)/shard_map/pallas_call | solution.py:151
  25.0 1.5 %collective-permute-start.4 = (f32[32,128]{1,0:T(8,128)}, f32[32,128]{1,0:T(8,128)S(1)}, u32[]{:S(2)}, u32[]{:S(2)}) collective-permute-start(f32[32,128]{1,0:T(8,128)} %get-tuple-element.19), channel_id=1, source_target_pairs={{0,252},{4,0},{8,4},{12,8},{16,12},{20,16},{24,20},{28,24},{32,28}... | collective-permute-start | bytes 49160 | tf_op jit(solution)/shard_map/ppermute | solution.py:17
  27.1 1.2 %collective-permute-done.4.right_ref = f32[32,128]{1,0:T(8,128)S(1)} collective-permute-done((f32[32,128]{1,0:T(8,128)}, f32[32,128]{1,0:T(8,128)S(1)}, u32[]{:S(2)}, u32[]{:S(2)}) %collective-permute-start.4) | collective-permute-done | bytes 16416 | tf_op jit(solution)/shard_map/ppermute | solution.py:17
  28.4 0.0 collective-permute-done.2.s3
  28.4 0.0 collective-permute-done.1.s2
  28.5 0.9 %copy-done.3 = f32[72,512]{1,0:T(8,128)S(1)} copy-done((f32[72,512]{1,0:T(8,128)S(1)}, f32[72,512]{1,0:T(8,128)}, u32[]{:S(2)}) %copy-start.3) | copy-done | bytes 147480
  29.4 0.7 %copy-done.5 = f32[32,128]{1,0:T(8,128)S(1)} copy-done((f32[32,128]{1,0:T(8,128)S(1)}, f32[32,128]{1,0:T(8,128)}, u32[]{:S(2)}) %copy-start.5) | copy-done | bytes 16408
  30.1 2.8 %shard_map.92 = (f32[64,1536]{1,0:T(8,128)S(1)}, f32[64,1024]{1,0:T(8,128)S(1)}) custom-call(s32[4]{0:T(128)S(1)} %copy-done.6, s32[1]{0:T(128)S(6)} %copy.10.counts_ref, f32[64,512]{1,0:T(8,128)S(1)} %copy-done.4, f32[64,512]{1,0:T(8,128)S(1)} %collective-permute-done.s1, f32[64,512]{1,0:T(8,128)S(1)} %collective-permute-done.1.s2, ...), custom_call_target="tpu_custom_call" | custom-call | flops 4000000000 | bytes 4000000 | tf_op jit(solution)/shard_map/pallas_call | solution.py:281
  32.9 6.3 %collective-permute-start.5 = (f32[64,1024]{1,0:T(8,128)S(1)}, f32[64,1024]{1,0:T(8,128)S(1)}, u32[]{:S(2)}, u32[]{:S(2)}) collective-permute-start(f32[64,1024]{1,0:T(8,128)S(1)} %get-tuple-element.21), channel_id=1, source_target_pairs={{0,4},{4,0},{8,12},{12,8},{16,20},{20,16},{24,28},{28,24},{32,36},... | collective-permute-start | bytes 786440 | tf_op jit(solution)/shard_map/ppermute | solution.py:21
  39.3 1.2 %collective-permute-done.5.got_ref = f32[64,1024]{1,0:T(8,128)S(1)} collective-permute-done((f32[64,1024]{1,0:T(8,128)S(1)}, f32[64,1024]{1,0:T(8,128)S(1)}, u32[]{:S(2)}, u32[]{:S(2)}) %collective-permute-start.5) | collective-permute-done | bytes 262176 | tf_op jit(solution)/shard_map/ppermute | solution.py:21
  40.5 0.1 collective-permute-start.6
  40.6 3.8 %collective-permute-start.7 = (f32[16,1536]{1,0:T(8,128)S(1)}, f32[16,1536]{1,0:T(8,128)S(1)}, u32[]{:S(2)}, u32[]{:S(2)}) collective-permute-start(f32[16,1536]{1,0:T(8,128)S(1)} %get-tuple-element.24), channel_id=1, source_target_pairs={{0,2},{1,3},{2,0},{3,1},{4,6},{5,7},{6,4},{7,5},{8,10},{9,11},{10,... | collective-permute-start | bytes 294920 | tf_op jit(solution)/shard_map/ppermute | solution.py:21
  44.4 0.1 collective-permute-done.6.b
  44.6 4.7 %collective-permute-done.7.c = f32[16,1536]{1,0:T(8,128)S(1)} collective-permute-done((f32[16,1536]{1,0:T(8,128)S(1)}, f32[16,1536]{1,0:T(8,128)S(1)}, u32[]{:S(2)}, u32[]{:S(2)}) %collective-permute-start.7) | collective-permute-done | bytes 98336 | tf_op jit(solution)/shard_map/ppermute | solution.py:21
  49.3 2.6 %collective-permute-done.8.d = f32[16,1536]{1,0:T(8,128)S(1)} collective-permute-done((f32[16,1536]{1,0:T(8,128)S(1)}, f32[16,1536]{1,0:T(8,128)S(1)}, u32[]{:S(2)}, u32[]{:S(2)}) %collective-permute-start.8) | collective-permute-done | bytes 98336 | tf_op jit(solution)/shard_map/ppermute | solution.py:21
  51.9 0.1 collective-permute-start.9
  52.0 3.6 %collective-permute-start.10 = (f32[16,512]{1,0:T(8,128)S(1)}, f32[16,512]{1,0:T(8,128)S(1)}, u32[]{:S(2)}, u32[]{:S(2)}) collective-permute-start(f32[16,512]{1,0:T(8,128)S(1)} %get-tuple-element.28), channel_id=1, source_target_pairs={{0,16},{4,20},{8,24},{12,28},{16,32},{20,36},{24,40},{28,44},{32,4... | collective-permute-start | bytes 98312 | tf_op jit(solution)/shard_map/ppermute | solution.py:17
  55.6 2.4 %collective-permute-done.9 = f32[16,512]{1,0:T(8,128)S(1)} collective-permute-done((f32[16,512]{1,0:T(8,128)S(1)}, f32[16,512]{1,0:T(8,128)S(1)}, u32[]{:S(2)}, u32[]{:S(2)}) %collective-permute-start.9) | collective-permute-done | bytes 32800 | tf_op jit(solution)/shard_map/ppermute | solution.py:17
  58.1 0.4 collective-permute-done.10
  58.5 0.6 %add_add_fusion = f32[16,512]{1,0:T(8,128)} fusion(f32[16,512]{1,0:T(8,128)S(1)} %collective-permute-done.10, f32[16,512]{1,0:T(8,128)S(1)} %get-tuple-element.26, f32[16,512]{1,0:T(8,128)S(1)} %collective-permute-done.9), kind=kLoop, calls=%fused_computation | loop fusion | flops 16384 | bytes 131072 | tf_op jit(solution)/shard_map/add | solution.py:362
  (20 shorter events, 0.1 us)
Async XLA Ops:
  0.0 28.4 %collective-permute-start.2 = (f32[64,512]{1,0:T(8,128)}, f32[64,512]{1,0:T(8,128)S(1)}, u32[]{:S(2)}, u32[]{:S(2)}) collective-permute-start(f32[64,512]{1,0:T(8,128)} %s0.1), channel_id=1, source_target_pairs={{0,244},{4,248},{8,252},{12,0},{16,4},{20,8},{24,12},{28,16},{32,2... | collective-permute-start | bytes 393224 | tf_op jit(solution)/shard_map/ppermute | solution.py:17
  9.2 19.2 %collective-permute-start.1 = (f32[64,512]{1,0:T(8,128)}, f32[64,512]{1,0:T(8,128)S(1)}, u32[]{:S(2)}, u32[]{:S(2)}) collective-permute-start(f32[64,512]{1,0:T(8,128)} %s0.1), channel_id=1, source_target_pairs={{0,248},{4,252},{8,0},{12,4},{16,8},{20,12},{24,16},{28,20},{32,24... | collective-permute-start | bytes 393224 | tf_op jit(solution)/shard_map/ppermute | solution.py:17
  9.7 18.7 %collective-permute-start = (f32[64,512]{1,0:T(8,128)}, f32[64,512]{1,0:T(8,128)S(1)}, u32[]{:S(2)}, u32[]{:S(2)}) collective-permute-start(f32[64,512]{1,0:T(8,128)} %s0.1), channel_id=1, source_target_pairs={{0,252},{4,0},{8,4},{12,8},{16,12},{20,16},{24,20},{28,24},{32,28}... | collective-permute-start | bytes 393224 | tf_op jit(solution)/shard_map/ppermute | solution.py:17
  10.4 18.0 %collective-permute-start.3 = (f32[64,512]{1,0:T(8,128)}, f32[64,512]{1,0:T(8,128)S(1)}, u32[]{:S(2)}, u32[]{:S(2)}) collective-permute-start(f32[64,512]{1,0:T(8,128)} %s0.1), channel_id=1, source_target_pairs={{0,240},{4,244},{8,248},{12,252},{16,0},{20,4},{24,8},{28,12},{32,... | collective-permute-start | bytes 393224 | tf_op jit(solution)/shard_map/ppermute | solution.py:17
  12.1 15.0 %copy-start.7 = (f32[4,256]{1,0:T(4,128)S(1)}, f32[4,256]{1,0:T(4,128)}, u32[]{:S(2)}) copy-start(f32[4,256]{1,0:T(4,128)} %param.11) | copy-start | bytes 12292
  12.1 16.3 %copy-start = (f32[32]{0:T(128)S(1)}, f32[32]{0:T(128)}, u32[]{:S(2)}) copy-start(f32[32]{0:T(128)} %param.16) | copy-start | bytes 388
  12.1 16.3 %copy-start.1 = (f32[32]{0:T(128)S(1)}, f32[32]{0:T(128)}, u32[]{:S(2)}) copy-start(f32[32]{0:T(128)} %param.17) | copy-start | bytes 388
  12.1 16.3 %copy-start.2 = (f32[4,64,2048]{2,1,0:T(8,128)S(1)}, f32[4,64,2048]{2,1,0:T(8,128)}, u32[]{:S(2)}) copy-start(f32[4,64,2048]{2,1,0:T(8,128)} %record_ref.1) | copy-start | bytes 6291460
  12.1 16.3 %copy-start.4 = (f32[64,512]{1,0:T(8,128)S(1)}, f32[64,512]{1,0:T(8,128)}, u32[]{:S(2)}) copy-start(f32[64,512]{1,0:T(8,128)} %s0.1) | copy-start | bytes 393220
  12.1 16.3 %copy-start.6 = (s32[4]{0:T(128)S(1)}, s32[4]{0:T(128)}, u32[]{:S(2)}) copy-start(s32[4]{0:T(128)} %offsets_ref.1) | copy-start | bytes 52
  25.0 3.4 %collective-permute-start.4 = (f32[32,128]{1,0:T(8,128)}, f32[32,128]{1,0:T(8,128)S(1)}, u32[]{:S(2)}, u32[]{:S(2)}) collective-permute-start(f32[32,128]{1,0:T(8,128)} %get-tuple-element.19), channel_id=1, source_target_pairs={{0,252},{4,0},{8,4},{12,8},{16,12},{20,16},{24,20},{28,24},{32,28}... | collective-permute-start | bytes 49160 | tf_op jit(solution)/shard_map/ppermute | solution.py:17
  28.4 0.9 %copy-start.3 = (f32[72,512]{1,0:T(8,128)S(1)}, f32[72,512]{1,0:T(8,128)}, u32[]{:S(2)}) copy-start(f32[72,512]{1,0:T(8,128)} %get-tuple-element.17.prior_ref) | copy-start | bytes 442372
  29.4 0.7 %copy-start.5 = (f32[32,128]{1,0:T(8,128)S(1)}, f32[32,128]{1,0:T(8,128)}, u32[]{:S(2)}) copy-start(f32[32,128]{1,0:T(8,128)} %get-tuple-element.18.left_ref) | copy-start | bytes 49156
  32.9 7.5 %collective-permute-start.5 = (f32[64,1024]{1,0:T(8,128)S(1)}, f32[64,1024]{1,0:T(8,128)S(1)}, u32[]{:S(2)}, u32[]{:S(2)}) collective-permute-start(f32[64,1024]{1,0:T(8,128)S(1)} %get-tuple-element.21), channel_id=1, source_target_pairs={{0,4},{4,0},{8,12},{12,8},{16,20},{20,16},{24,28},{28,24},{32,36},... | collective-permute-start | bytes 786440 | tf_op jit(solution)/shard_map/ppermute | solution.py:21
  40.5 4.1 %collective-permute-start.6 = (f32[16,1536]{1,0:T(8,128)S(1)}, f32[16,1536]{1,0:T(8,128)S(1)}, u32[]{:S(2)}, u32[]{:S(2)}) collective-permute-start(f32[16,1536]{1,0:T(8,128)S(1)} %get-tuple-element.23), channel_id=1, source_target_pairs={{0,1},{1,0},{2,3},{3,2},{4,5},{5,4},{6,7},{7,6},{8,9},{9,8},{10,11... | collective-permute-start | bytes 294920 | tf_op jit(solution)/shard_map/ppermute | solution.py:21
  40.6 8.7 %collective-permute-start.7 = (f32[16,1536]{1,0:T(8,128)S(1)}, f32[16,1536]{1,0:T(8,128)S(1)}, u32[]{:S(2)}, u32[]{:S(2)}) collective-permute-start(f32[16,1536]{1,0:T(8,128)S(1)} %get-tuple-element.24), channel_id=1, source_target_pairs={{0,2},{1,3},{2,0},{3,1},{4,6},{5,7},{6,4},{7,5},{8,10},{9,11},{10,... | collective-permute-start | bytes 294920 | tf_op jit(solution)/shard_map/ppermute | solution.py:21
  44.4 7.5 %collective-permute-start.8 = (f32[16,1536]{1,0:T(8,128)S(1)}, f32[16,1536]{1,0:T(8,128)S(1)}, u32[]{:S(2)}, u32[]{:S(2)}) collective-permute-start(f32[16,1536]{1,0:T(8,128)S(1)} %get-tuple-element.25), channel_id=1, source_target_pairs={{0,3},{1,2},{2,1},{3,0},{4,7},{5,6},{6,5},{7,4},{8,11},{9,10},{10,... | collective-permute-start | bytes 294920 | tf_op jit(solution)/shard_map/ppermute | solution.py:21
  51.9 6.2 %collective-permute-start.9 = (f32[16,512]{1,0:T(8,128)S(1)}, f32[16,512]{1,0:T(8,128)S(1)}, u32[]{:S(2)}, u32[]{:S(2)}) collective-permute-start(f32[16,512]{1,0:T(8,128)S(1)} %get-tuple-element.27), channel_id=1, source_target_pairs={{0,8},{4,12},{8,16},{12,20},{16,24},{20,28},{24,32},{28,36},{32,40... | collective-permute-start | bytes 98312 | tf_op jit(solution)/shard_map/ppermute | solution.py:17
  52.0 6.5 %collective-permute-start.10 = (f32[16,512]{1,0:T(8,128)S(1)}, f32[16,512]{1,0:T(8,128)S(1)}, u32[]{:S(2)}, u32[]{:S(2)}) collective-permute-start(f32[16,512]{1,0:T(8,128)S(1)} %get-tuple-element.28), channel_id=1, source_target_pairs={{0,16},{4,20},{8,24},{12,28},{16,32},{20,36},{24,40},{28,44},{32,4... | collective-permute-start | bytes 98312 | tf_op jit(solution)/shard_map/ppermute | solution.py:17

commit v2 on v1

v2 whole, which is shorter than its diff:
```python
import functools

import jax
import jax.numpy as jnp
from jax import lax
from jax.experimental import pallas as pl
from jax.experimental.pallas import tpu as pltpu
from jax.sharding import PartitionSpec as P

F32 = jnp.float32
BF16 = jnp.bfloat16
LANES = 128


def shifted(x, axis, by):
    length = lax.axis_size(axis)
    return lax.ppermute(x, axis, [(i, (i + by) % length) for i in range(length)])


def partner(x, axis, mask):
    return lax.ppermute(x, axis, [(i, i ^ mask) for i in range(lax.axis_size(axis))])


def lane_index(shape):
    return lax.broadcasted_iota(jnp.int32, shape, 1)


def column(row):
    n = row.shape[1]
    spread = jnp.broadcast_to(row, (n, n))
    diagonal = lax.broadcasted_iota(jnp.int32, (n, n), 0) == lane_index((n, n))
    return jnp.sum(jnp.where(diagonal, spread, 0.0), axis=1, keepdims=True)


def weighted_silu(hidden, half_weight):
    return hidden * (1.0 + jnp.tanh(0.5 * hidden)) * half_weight


def gather_rows(sums):
    sub = lax.broadcasted_iota(jnp.int32, sums[0].shape, 0)
    half = sub < 4
    first = [
        jnp.where(half, sums[i], sums[i + 4]) + pltpu.roll(jnp.where(half, sums[i + 4], sums[i]), 4, 0)
        for i in range(4)
    ]
    low = (sub & 2) == 0
    second = [
        jnp.where(low, first[i] + pltpu.roll(first[i], 6, 0), first[i + 2] + pltpu.roll(first[i + 2], 2, 0))
        for i in range(2)
    ]
    even = (sub & 1) == 0
    return jnp.where(even, second[0] + pltpu.roll(second[0], 7, 0), second[1] + pltpu.roll(second[1], 1, 0))


def conv_kernel(w_ref, bias_ref, ow_ref, *refs):
    x_refs, (prior_ref, own_ref, send_ref, t_ref, a_ref, b_ref) = refs[:-6], refs[-6:]
    step = pl.program_id(0)
    channels = w_ref.shape[1]
    cols = prior_ref.shape[1]
    outs = bias_ref.shape[1]
    taps = 3 * outs
    block = 8
    pairs = block // 2
    strip_rows = prior_ref.shape[0] - block

    @pl.when(step == 0)
    def _():
        w = [w_ref[a * taps : (a + 1) * taps, :] for a in range(3)]
        none = jnp.zeros_like(w[0])
        for j, (even, odd) in enumerate(((w[2], none), (w[1], w[2]), (w[0], w[1]), (none, w[0]))):
            t_ref[j * taps : (j + 1) * taps, :channels] = even
            t_ref[j * taps : (j + 1) * taps, channels:] = odd
        b_ref[pairs - 1] = jnp.zeros(b_ref.shape[1:], F32)
        own_ref[...] = jnp.zeros_like(own_ref)
        send_ref[...] = jnp.zeros_like(send_ref)

    bias = column(jnp.concatenate([bias_ref[...]] * 2, axis=1))
    half_weight = column(jnp.concatenate([ow_ref[...]] * 2, axis=1)) * 0.5
    lane = lane_index((2 * outs, LANES))
    col = lane_index((block, cols))
    inner = jnp.logical_and(col > 0, col < cols - 1)

    def load(half):
        parts = [jnp.swapaxes(x[:, half * block : (half + 1) * block, :], 0, 1) for x in x_refs]
        return jnp.concatenate(parts, axis=1)

    def multiply(p_ref, x, pair):
        both = x[2 * pair : 2 * pair + 2].reshape(2 * channels, cols)
        p_ref[pair] = jnp.dot(t_ref[...], both, preferred_element_type=F32)

    def two_rows(batch, *terms):
        sums, edges = batch
        both = sum(p_ref[pair, j * taps : (j + 2) * taps, :] for p_ref, pair, j in terms)

        def tap(b):
            return jnp.concatenate([both[n * taps + b * outs : n * taps + (b + 1) * outs] for n in range(2)], axis=0)

        tail = cols - LANES
        before = pltpu.roll(tap(0), 1, 1)
        after = pltpu.roll(tap(2), cols - 1, 1)
        here = tap(1)
        score = weighted_silu(before + here + after + bias, half_weight)
        own = jnp.where(lane == 0, here[:, :LANES] + after[:, :LANES], here[:, tail:] + before[:, tail:])
        send = jnp.where(lane == 0, before[:, :LANES], after[:, tail:])
        for n in range(2):
            i = len(sums)
            cut = slice(n * outs, (n + 1) * outs)
            sums.append(sum(score[n * outs + k : n * outs + k + 8] for k in range(0, outs, 8)))
            mine = (lane[cut] >> 1) == i
            for m, ends in enumerate((own[cut], send[cut])):
                edges[m] = jnp.where(mine, pltpu.roll(ends, 2 * i + 1, 1), edges[m])

    def new_batch():
        return [], [jnp.zeros((outs, LANES), F32)] * 2

    def store(batch, base):
        sums, edges = batch
        prior_ref[pl.ds(pl.multiple_of(base, block), block), :] = jnp.where(inner, gather_rows(sums), 0.0)
        row = base - (block - 1) + (lane[:outs] >> 1)
        valid = jnp.logical_and(row >= 0, row < strip_rows)
        turn = (2 * base + LANES - 2 * (block - 1)) % LANES
        for ref, ends in zip((own_ref, send_ref), edges):
            ref[...] += pltpu.roll(jnp.where(valid, ends, 0.0), turn, 1)

    def inner_rows(batch, p_ref, pair):
        two_rows(batch, (p_ref, pair, 2), (p_ref, pair + 1, 0))

    def phase(p_ref, earlier_ref, half, base):
        x = load(half)
        batch = new_batch()
        for pair in range(pairs):
            multiply(p_ref, x, pair)
            if pair < pairs - 1:
                inner_rows(batch, earlier_ref, pair)
        two_rows(batch, (earlier_ref, pairs - 1, 2), (p_ref, 0, 0))
        store(batch, base)

    start = step * 2 * block
    phase(a_ref, b_ref, 0, start)
    phase(b_ref, a_ref, 1, start + block)

    @pl.when(step == pl.num_programs(0) - 1)
    def _():
        batch = new_batch()
        for pair in range(pairs - 1):
            inner_rows(batch, b_ref, pair)
        two_rows(batch, (b_ref, pairs - 1, 2))
        store(batch, strip_rows)


def far(x):
    return pltpu.with_memory_space_constraint(x, pltpu.HBM)


def conv_prior(features, weight, bias, out_weight):
    channels, strip_rows, cols = features.shape
    outs = bias.shape[0]
    block = 8
    taps = 3 * outs
    cuts = 4
    flat = weight.transpose(1, 2, 0, 3).reshape(9 * outs, channels)
    full = lambda shape: pl.BlockSpec(shape, lambda i: (0,) * len(shape))
    return pl.pallas_call(
        conv_kernel,
        grid=(strip_rows // (2 * block),),
        in_specs=[full((9 * outs, channels)), full((1, outs)), full((1, outs))]
        + [
            pl.BlockSpec((channels // cuts, 2 * block, cols), functools.partial(lambda n, i: (n, i, 0), n))
            for n in range(cuts)
        ],
        out_specs=[full((strip_rows + block, cols)), full((outs, LANES)), full((outs, LANES))],
        out_shape=[
            jax.ShapeDtypeStruct((strip_rows + block, cols), F32),
            jax.ShapeDtypeStruct((outs, LANES), F32),
            jax.ShapeDtypeStruct((outs, LANES), F32),
        ],
        scratch_shapes=[
            pltpu.VMEM((4 * taps, 2 * channels), BF16),
            pltpu.VMEM((block // 2, 4 * taps, cols), F32),
            pltpu.VMEM((block // 2, 4 * taps, cols), F32),
        ],
        compiler_params=pltpu.CompilerParams(vmem_limit_bytes=32 << 20),
        cost_estimate=pl.CostEstimate(flops=8_000_000_000, bytes_accessed=9_000_000, transcendentals=1_000_000),
    )(*[far(x) for x in (flat, bias.reshape(1, outs), out_weight.reshape(1, outs))], *([far(features)] * cuts))


def split(x):
    high = x.astype(BF16)
    return high, (x - high.astype(F32)).astype(BF16)


def exposure_kernel(
    offsets_ref, counts_ref, s0, s1, s2, s3, s4, record_ref, taps_ref, send_ref, keep_ref, give_ref, ext_ref, acc_ref
):
    slots, rows, width = record_ref.shape
    cols = s0.shape[1]
    tap_count = taps_ref.shape[2]
    pieces = width // tap_count
    tiles = width // LANES
    per = tap_count // LANES
    for d, part in enumerate((s0, s1, s2, s3, s4)):
        ext_ref[:, d * cols : (d + 1) * cols] = part[...]
    acc_ref[...] = jnp.zeros_like(acc_ref)

    def add_slot(n):
        offset = offsets_ref[n]
        rest = offset % LANES
        base = pl.multiple_of(offset - rest, LANES)
        lane = lane_index((rows, LANES))

        taps = taps_ref[n]
        wide = jnp.concatenate([taps, jnp.zeros_like(taps)], axis=1)
        band = pltpu.roll(jnp.broadcast_to(wide, (tap_count, 2 * tap_count)), 0, 1, stride=1, stride_axis=0)
        first, second = split(band[:, :tap_count]), split(band[:, tap_count:])

        def banded(x, turn, axis):
            high, low = split(x)
            part_high, part_low = [jnp.concatenate(pair, axis=1 - axis) for pair in zip(first, second)]
            both = lax.dot_general(
                jnp.concatenate([high, low, high], axis=1),
                jnp.concatenate([part_high, part_high, part_low], axis=axis),
                (((1,), (axis,)), ((), ())),
                preferred_element_type=F32,
            )
            k = turn * rows % x.shape[0]
            return both[:, :tap_count] + jnp.concatenate([both[k:, tap_count:], both[:k, tap_count:]], axis=0)

        turned = [
            pltpu.roll(ext_ref[:, pl.ds(base + m * LANES, LANES)], LANES - rest, 1) for m in range(tiles + 1)
        ]
        keep = lane < LANES - rest
        window = [jnp.where(keep, turned[m], turned[m + 1]) for m in range(tiles)]
        stacked = jnp.concatenate(
            [jnp.concatenate(window[p * per : (p + 1) * per], axis=1) for p in range(pieces)], axis=0
        )
        record = jnp.concatenate(
            [record_ref[n, :, p * tap_count : (p + 1) * tap_count] for p in range(pieces)], axis=0
        )
        live = jnp.where(counts_ref[...] > n, 1.0, 0.0)
        residual = (record - banded(stacked, pieces - 1, 0)) * live
        back = banded(residual, 1, 1)
        moved = []
        for m in range(tiles):
            p, h = divmod(m, per)
            moved.append(pltpu.roll(back[p * rows : (p + 1) * rows, h * LANES : (h + 1) * LANES], rest, 1))
        nothing = jnp.zeros((rows, LANES), F32)
        spill = lane < rest
        for m in range(tiles + 1):
            inside = moved[m] if m < tiles else nothing
            earlier = moved[m - 1] if m > 0 else nothing
            acc_ref[:, pl.ds(base + m * LANES, LANES)] += jnp.where(spill, earlier, inside)

    for n in range(slots):
        add_slot(n)

    for d in range(5):
        to_ref = give_ref if d % 2 else keep_ref
        to_ref[:, d // 2 * cols : (d // 2 + 1) * cols] = acc_ref[:, d * cols : (d + 1) * cols]
    outs = send_ref.shape[0]
    give_ref[:outs, 2 * cols :] = send_ref[...]
    give_ref[outs:, 2 * cols :] = jnp.zeros((rows - outs, LANES), F32)


def exposure_terms(offsets, counts, sky_parts, exposures, psf_taps, send):
    slots, rows, width = exposures.shape
    cols = sky_parts[0].shape[1]
    reach = len(sky_parts) * cols
    keep = (rows, 3 * cols)
    give = (rows, 2 * cols + LANES)
    near = pl.BlockSpec(memory_space=pltpu.VMEM)
    few = pl.BlockSpec(memory_space=pltpu.SMEM)
    return pl.pallas_call(
        exposure_kernel,
        in_specs=[few] + [near] * (len(sky_parts) + 4),
        out_specs=[near] * 2,
        out_shape=[jax.ShapeDtypeStruct(keep, F32), jax.ShapeDtypeStruct(give, F32)],
        scratch_shapes=[pltpu.VMEM((rows, reach), F32), pltpu.VMEM((rows, reach), F32)],
        compiler_params=pltpu.CompilerParams(vmem_limit_bytes=32 << 20),
        cost_estimate=pl.CostEstimate(flops=6_000_000_000, bytes_accessed=4_000_000, transcendentals=0),
    )(offsets, counts.reshape(1, 1), *sky_parts, exposures, psf_taps.reshape(slots, 1, -1), send)


def join_kernel(keep_ref, got_ref, cross_ref, prior_ref, own_ref, bias_ref, ow_ref, *outs):
    outs, full_ref = outs[:-1], outs[-1]
    second = lax.axis_index("sky") % 2 == 1
    group = lax.axis_index("grp")
    share, width = outs[0].shape
    cols = width // 3
    rows = keep_ref.shape[0]
    channels = own_ref.shape[0]
    lane = lane_index((channels, LANES))
    beside = got_ref[:channels, 2 * cols :]
    from_beside = jnp.logical_xor((lane & 1) == 0, second)
    edge = own_ref[...] + jnp.where(from_beside, beside, cross_ref[...]) + column(bias_ref[...])
    score = jnp.sum(weighted_silu(edge, column(ow_ref[...]) * 0.5), axis=0, keepdims=True)
    lane = lane_index((rows, LANES))
    mine = jnp.where((lane >> 1) == lax.broadcasted_iota(jnp.int32, (rows, LANES), 0), score, 0.0)
    last = jnp.sum(jnp.where((lane & 1) == 0, mine, 0.0), axis=1, keepdims=True)
    first = jnp.sum(jnp.where((lane & 1) == 1, mine, 0.0), axis=1, keepdims=True)
    col = lane_index((rows, cols))
    skipped = prior_ref.shape[0] - rows - 1
    full_ref[...] = (
        keep_ref[:, :cols]
        + prior_ref[skipped : skipped + rows, :]
        + jnp.where(col == 0, first, 0.0)
        + jnp.where(col == cols - 1, last, 0.0)
    )
    for k, out in enumerate(outs):
        top = pl.ds(pl.multiple_of((group ^ k) * share, share), share)
        low = got_ref[top, :cols]
        high = got_ref[top, cols : 2 * cols]
        out[:, :cols] = full_ref[top, :] + jnp.where(second, low, 0.0)
        out[:, cols : 2 * cols] = keep_ref[top, cols : 2 * cols] + jnp.where(second, high, low)
        out[:, 2 * cols :] = keep_ref[top, 2 * cols :] + jnp.where(second, 0.0, high)


def sum_kernel(a, b, c, d, *outs):
    cols = outs[0].shape[1]
    for k, out in enumerate(outs):
        cut = slice(k * cols, (k + 1) * cols)
        out[...] = (a[:, cut] + b[:, cut]) + (c[:, cut] + d[:, cut])


def small_call(kernel, out_shapes, *operands, scratch=()):
    near = pl.BlockSpec(memory_space=pltpu.VMEM)
    return pl.pallas_call(
        kernel,
        in_specs=[near] * len(operands),
        out_specs=[near] * len(out_shapes),
        out_shape=[jax.ShapeDtypeStruct(shape, F32) for shape in out_shapes],
        scratch_shapes=[pltpu.VMEM(shape, F32) for shape in scratch],
        compiler_params=pltpu.CompilerParams(vmem_limit_bytes=8 << 20),
        cost_estimate=pl.CostEstimate(flops=200_000, bytes_accessed=1_000_000, transcendentals=0),
    )(*operands)


def on_device(
    sky_strip, exposures, psf_taps, offsets, counts, features, conv_weight, conv_bias, out_weight
):
    n_grp = lax.axis_size("grp")
    strip_rows, cols = sky_strip.shape
    share = strip_rows // n_grp
    reach_blocks = exposures.shape[2] // cols
    parts = [sky_strip]
    for distance in range(1, reach_blocks + 1):
        parts.append(shifted(sky_strip, "sky", -distance))
    prior, own_edge, send = conv_prior(features, conv_weight, conv_bias, out_weight)
    n_sky = lax.axis_size("sky")
    cross = lax.ppermute(send, "sky", [(i, (i - 1 if i % 2 == 0 else i + 1) % n_sky) for i in range(n_sky)])
    keep, give = exposure_terms(offsets, counts, parts, exposures, psf_taps, send)
    give, cross = lax.optimization_barrier((give, cross))
    got = partner(give, "sky", 1)
    terms = small_call(
        join_kernel, [(share, 3 * cols)] * n_grp, keep, got, cross, prior, own_edge,
        conv_bias.reshape(1, -1), out_weight.reshape(1, -1), scratch=[(strip_rows, cols)],
    )
    received = [terms[0]] + [partner(terms[k], "grp", k) for k in range(1, n_grp)]
    own, near, far = small_call(sum_kernel, [(share, cols)] * 3, *received)
    return own + shifted(near, "sky", 2) + shifted(far, "sky", 4)


def solution(mesh):
    placed = (
        P(None, "sky"),
        P(("sky", "grp"), None, None),
        P(("sky", "grp"), None),
        P(("sky", "grp")),
        P(("sky", "grp")),
        P(None, None, "sky"),
        P("grp", None, None, None),
        P("grp"),
        P("grp"),
    )
    return jax.shard_map(
        on_device, mesh=mesh, in_specs=placed, out_specs=P("grp", "sky"), check_vma=False
    )
```

time: 58.8 us -> 50.4 us (0.86)
  starting transfers between devices: 27.6 us -> 21.8 us
  local copies, waits for them, and re-layouts: 1.65 us -> 0.03 us
  Pallas kernels: 15.8 us -> 15 us
  waiting for transfers between devices: 12.7 us -> 12.1 us
    ppermute x4, starting transfers between devices: 10.3 us -> 5.63 us  [partner(): lax.ppermute(x, axis, [(i, i ^ mask) for i in range(lax.axis_size(axis))])]
    pallas_call x1, Pallas kernels: 12.9 us -> 9.5 us  [conv_prior(): pl.pallas_call(conv_kernel, grid=(strip_rows // (2 * block),), in_specs=[...]
    pallas_call x1, Pallas kernels: 2.84 us -> 5.28 us  [exposure_terms(): pl.pallas_call(exposure_kernel, in_specs=[few] + [near] * (len(sky_parts)...]
    unnamed x16 -> x12, local copies, waits for them, and re-layouts: 1.64 us -> 0.03 us
    ppermute x7 -> x6, starting transfers between devices: 17.3 us -> 16.1 us  [shifted(): lax.ppermute(x, axis, [(i, (i + by) % length) for i in range(length)])]
    ppermute x7 -> x6, waiting for transfers between devices: 4.06 us -> 3.67 us  [shifted(): lax.ppermute(x, axis, [(i, (i + by) % length) for i in range(length)])]
  transfers between devices with their start and end apart: 11 -> 11, of which waited for: 7 -> 6; matrix products, arithmetic and copies ran while one was open for 0% -> 0% of each run, Pallas kernels for 22% -> 29%
where the time goes in v2:
time: 50.4 us
  starting transfers between devices  21.8 us (43%)
  Pallas kernels  15 us (30%)
  waiting for transfers between devices  12.1 us (24%)
  between operations  0.79 us (2%)
  other arithmetic  0.62 us (1%)
    ppermute x6, starting transfers between devices, shifted(): lax.ppermute(x, axis, [(i, (i + by) % length) for i in range(length)])  16.1 us
    pallas_call x1, Pallas kernels, conv_prior(): pl.pallas_call(conv_kernel, grid=(strip_rows // (2 * block),), in_specs=[...  9.5 us
    ppermute x4, waiting for transfers between devices, partner(): lax.ppermute(x, axis, [(i, i ^ mask) for i in range(lax.axis_size(axis))])  8.44 us
    ppermute x4, starting transfers between devices, partner(): lax.ppermute(x, axis, [(i, i ^ mask) for i in range(lax.axis_size(axis))])  5.63 us
    pallas_call x1, Pallas kernels, exposure_terms(): pl.pallas_call(exposure_kernel, in_specs=[few] + [near] * (len(sky_parts)...  5.28 us
    ppermute x6, waiting for transfers between devices, shifted(): lax.ppermute(x, axis, [(i, (i + by) % length) for i in range(length)])  3.67 us
  transfers between devices with their start and end apart: 11, of which 6 were waited for; matrix products, arithmetic and copies ran while one was open for 0% of the time, Pallas kernels for 29%

profile of v2, /device:TPU:1, one launch (start us, length us, event | category | flops | bytes accessed | tf_op | source)
XLA Modules:
  0.0 50.4 jit_solution(15425829995525588356)
XLA Ops:
  0.0 3.2 %collective-permute-start = (f32[64,512]{1,0:T(8,128)}, f32[64,512]{1,0:T(8,128)S(1)}, u32[]{:S(2)}, u32[]{:S(2)}) collective-permute-start(f32[64,512]{1,0:T(8,128)} %s0.1), channel_id=1, source_target_pairs={{0,252},{4,0},{8,4},{12,8},{16,12},{20,16},{24,20},{28,24},{32,28}... | collective-permute-start | bytes 393224 | tf_op jit(solution)/shard_map/ppermute | solution.py:17
  3.2 6.0 %collective-permute-start.1 = (f32[64,512]{1,0:T(8,128)}, f32[64,512]{1,0:T(8,128)S(1)}, u32[]{:S(2)}, u32[]{:S(2)}) collective-permute-start(f32[64,512]{1,0:T(8,128)} %s0.1), channel_id=1, source_target_pairs={{0,248},{4,252},{8,0},{12,4},{16,8},{20,12},{24,16},{28,20},{32,24... | collective-permute-start | bytes 393224 | tf_op jit(solution)/shard_map/ppermute | solution.py:17
  9.3 0.7 %collective-permute-start.2 = (f32[64,512]{1,0:T(8,128)}, f32[64,512]{1,0:T(8,128)S(1)}, u32[]{:S(2)}, u32[]{:S(2)}) collective-permute-start(f32[64,512]{1,0:T(8,128)} %s0.1), channel_id=1, source_target_pairs={{0,244},{4,248},{8,252},{12,0},{16,4},{20,8},{24,12},{28,16},{32,2... | collective-permute-start | bytes 393224 | tf_op jit(solution)/shard_map/ppermute | solution.py:17
  10.0 2.9 %collective-permute-start.3 = (f32[64,512]{1,0:T(8,128)}, f32[64,512]{1,0:T(8,128)S(1)}, u32[]{:S(2)}, u32[]{:S(2)}) collective-permute-start(f32[64,512]{1,0:T(8,128)} %s0.1), channel_id=1, source_target_pairs={{0,240},{4,244},{8,248},{12,252},{16,0},{20,4},{24,8},{28,12},{32,... | collective-permute-start | bytes 393224 | tf_op jit(solution)/shard_map/ppermute | solution.py:17
  12.9 9.5 %shard_map.91 = (f32[72,512]{1,0:T(8,128)S(1)}, f32[32,128]{1,0:T(8,128)S(1)}, f32[32,128]{1,0:T(8,128)S(1)}) custom-call(bf16[288,128]{1,0:T(8,128)(2,1)} %bitcast.11, f32[1,32]{1,0:T(1,128)} %bitcast.7, f32[1,32]{1,0:T(1,128)} %bitcast.9, bf16[128,64,512]{2,1,0:T(8,128)(2,1)} %refs_3_.1, bf16[128,64,512]{2,1,0:T(8,128)(2,1)} %refs_3_.1, ...), custom_call_target="tpu_custom_call" | custom-call | flops 8000000000 | bytes 9000000 | tf_op jit(solution)/shard_map/pallas_call | solution.py:163
  22.4 0.1 collective-permute-start.4
  23.1 0.0 collective-permute-done.s1
  23.2 0.0 collective-permute-done.1.s2
  23.2 0.0 copy-start
  23.2 0.0 copy-start.1
  23.2 5.3 %shard_map.92 = (f32[64,1536]{1,0:T(8,128)S(1)}, f32[64,1152]{1,0:T(8,128)S(1)}) custom-call(s32[4]{0:T(128)S(1)} %copy-done.4, s32[1,1]{1,0:T(1,128)} %bitcast.6.counts_ref, f32[64,512]{1,0:T(8,128)S(1)} %copy-done.3, f32[64,512]{1,0:T(8,128)S(1)} %collective-permute-done.s1, f32[64,512]{1,0:T(8,128)S(1)} %collective-permute-done.1.s2, ...), custom_call_target="tpu_custom_call" | custom-call | flops 6000000000 | bytes 4000000 | tf_op jit(solution)/shard_map/pallas_call | solution.py:272
  28.5 1.6 %collective-permute-start.5 = (f32[64,1152]{1,0:T(8,128)S(1)}, f32[64,1152]{1,0:T(8,128)S(1)}, u32[]{:S(2)}, u32[]{:S(2)}) collective-permute-start(f32[64,1152]{1,0:T(8,128)S(1)} %get-tuple-element.22), channel_id=1, source_target_pairs={{0,4},{4,0},{8,12},{12,8},{16,20},{20,16},{24,28},{28,24},{32,36},... | collective-permute-start | bytes 884744 | tf_op jit(solution)/shard_map/ppermute | solution.py:21
  30.2 1.2 %collective-permute-done.5.got_ref = f32[64,1152]{1,0:T(8,128)S(1)} collective-permute-done((f32[64,1152]{1,0:T(8,128)S(1)}, f32[64,1152]{1,0:T(8,128)S(1)}, u32[]{:S(2)}, u32[]{:S(2)}) %collective-permute-start.5) | collective-permute-done | bytes 294944 | tf_op jit(solution)/shard_map/ppermute | solution.py:21
  31.4 0.2 shard_map.93
  31.6 1.4 %collective-permute-start.6 = (f32[16,1536]{1,0:T(8,128)S(1)}, f32[16,1536]{1,0:T(8,128)S(1)}, u32[]{:S(2)}, u32[]{:S(2)}) collective-permute-start(f32[16,1536]{1,0:T(8,128)S(1)} %get-tuple-element.27), channel_id=1, source_target_pairs={{0,1},{1,0},{2,3},{3,2},{4,5},{5,4},{6,7},{7,6},{8,9},{9,8},{10,11... | collective-permute-start | bytes 294920 | tf_op jit(solution)/shard_map/ppermute | solution.py:21
  33.0 2.6 %collective-permute-start.7 = (f32[16,1536]{1,0:T(8,128)S(1)}, f32[16,1536]{1,0:T(8,128)S(1)}, u32[]{:S(2)}, u32[]{:S(2)}) collective-permute-start(f32[16,1536]{1,0:T(8,128)S(1)} %get-tuple-element.28), channel_id=1, source_target_pairs={{0,2},{1,3},{2,0},{3,1},{4,6},{5,7},{6,4},{7,5},{8,10},{9,11},{10,... | collective-permute-start | bytes 294920 | tf_op jit(solution)/shard_map/ppermute | solution.py:21
  35.6 0.1 collective-permute-done.6.b
  35.7 4.6 %collective-permute-done.7.c = f32[16,1536]{1,0:T(8,128)S(1)} collective-permute-done((f32[16,1536]{1,0:T(8,128)S(1)}, f32[16,1536]{1,0:T(8,128)S(1)}, u32[]{:S(2)}, u32[]{:S(2)}) %collective-permute-start.7) | collective-permute-done | bytes 98336 | tf_op jit(solution)/shard_map/ppermute | solution.py:21
  40.2 2.6 %collective-permute-done.8.d = f32[16,1536]{1,0:T(8,128)S(1)} collective-permute-done((f32[16,1536]{1,0:T(8,128)S(1)}, f32[16,1536]{1,0:T(8,128)S(1)}, u32[]{:S(2)}, u32[]{:S(2)}) %collective-permute-start.8) | collective-permute-done | bytes 98336 | tf_op jit(solution)/shard_map/ppermute | solution.py:21
  42.9 0.8 %collective-permute-start.10 = (f32[16,512]{1,0:T(8,128)S(1)}, f32[16,512]{1,0:T(8,128)S(1)}, u32[]{:S(2)}, u32[]{:S(2)}) collective-permute-start(f32[16,512]{1,0:T(8,128)S(1)} %get-tuple-element.32), channel_id=1, source_target_pairs={{0,16},{4,20},{8,24},{12,28},{16,32},{20,36},{24,40},{28,44},{32,4... | collective-permute-start | bytes 98312 | tf_op jit(solution)/shard_map/ppermute | solution.py:17
  43.7 2.4 %collective-permute-start.9 = (f32[16,512]{1,0:T(8,128)S(1)}, f32[16,512]{1,0:T(8,128)S(1)}, u32[]{:S(2)}, u32[]{:S(2)}) collective-permute-start(f32[16,512]{1,0:T(8,128)S(1)} %get-tuple-element.31), channel_id=1, source_target_pairs={{0,8},{4,12},{8,16},{12,20},{16,24},{20,28},{24,32},{28,36},{32,40... | collective-permute-start | bytes 98312 | tf_op jit(solution)/shard_map/ppermute | solution.py:17
  46.1 3.2 %collective-permute-done.10 = f32[16,512]{1,0:T(8,128)S(1)} collective-permute-done((f32[16,512]{1,0:T(8,128)S(1)}, f32[16,512]{1,0:T(8,128)S(1)}, u32[]{:S(2)}, u32[]{:S(2)}) %collective-permute-start.10) | collective-permute-done | bytes 32800 | tf_op jit(solution)/shard_map/ppermute | solution.py:17
  49.3 0.4 collective-permute-done.9
  49.7 0.6 %add_add_fusion = f32[16,512]{1,0:T(8,128)} fusion(f32[16,512]{1,0:T(8,128)S(1)} %collective-permute-done.10, f32[16,512]{1,0:T(8,128)S(1)} %get-tuple-element.30, f32[16,512]{1,0:T(8,128)S(1)} %collective-permute-done.9), kind=kLoop, calls=%fused_computation | loop fusion | flops 16384 | bytes 131072 | tf_op jit(solution)/shard_map/add | solution.py:359
  (16 shorter events, 0.1 us)
Async XLA Ops:
  0.0 23.1 %collective-permute-start = (f32[64,512]{1,0:T(8,128)}, f32[64,512]{1,0:T(8,128)S(1)}, u32[]{:S(2)}, u32[]{:S(2)}) collective-permute-start(f32[64,512]{1,0:T(8,128)} %s0.1), channel_id=1, source_target_pairs={{0,252},{4,0},{8,4},{12,8},{16,12},{20,16},{24,20},{28,24},{32,28}... | collective-permute-start | bytes 393224 | tf_op jit(solution)/shard_map/ppermute | solution.py:17
  3.2 19.9 %collective-permute-start.1 = (f32[64,512]{1,0:T(8,128)}, f32[64,512]{1,0:T(8,128)S(1)}, u32[]{:S(2)}, u32[]{:S(2)}) collective-permute-start(f32[64,512]{1,0:T(8,128)} %s0.1), channel_id=1, source_target_pairs={{0,248},{4,252},{8,0},{12,4},{16,8},{20,12},{24,16},{28,20},{32,24... | collective-permute-start | bytes 393224 | tf_op jit(solution)/shard_map/ppermute | solution.py:17
  9.3 13.9 %collective-permute-start.2 = (f32[64,512]{1,0:T(8,128)}, f32[64,512]{1,0:T(8,128)S(1)}, u32[]{:S(2)}, u32[]{:S(2)}) collective-permute-start(f32[64,512]{1,0:T(8,128)} %s0.1), channel_id=1, source_target_pairs={{0,244},{4,248},{8,252},{12,0},{16,4},{20,8},{24,12},{28,16},{32,2... | collective-permute-start | bytes 393224 | tf_op jit(solution)/shard_map/ppermute | solution.py:17
  10.0 13.2 %collective-permute-start.3 = (f32[64,512]{1,0:T(8,128)}, f32[64,512]{1,0:T(8,128)S(1)}, u32[]{:S(2)}, u32[]{:S(2)}) collective-permute-start(f32[64,512]{1,0:T(8,128)} %s0.1), channel_id=1, source_target_pairs={{0,240},{4,244},{8,248},{12,252},{16,0},{20,4},{24,8},{28,12},{32,... | collective-permute-start | bytes 393224 | tf_op jit(solution)/shard_map/ppermute | solution.py:17
  12.9 9.6 %copy-start.5 = (f32[4,256]{1,0:T(4,128)S(1)}, f32[4,256]{1,0:T(4,128)}, u32[]{:S(2)}) copy-start(f32[4,256]{1,0:T(4,128)} %param.11) | copy-start | bytes 12292
  12.9 10.3 %copy-start.2 = (f32[4,64,2048]{2,1,0:T(8,128)S(1)}, f32[4,64,2048]{2,1,0:T(8,128)}, u32[]{:S(2)}) copy-start(f32[4,64,2048]{2,1,0:T(8,128)} %record_ref.1) | copy-start | bytes 6291460
  12.9 10.3 %copy-start.3 = (f32[64,512]{1,0:T(8,128)S(1)}, f32[64,512]{1,0:T(8,128)}, u32[]{:S(2)}) copy-start(f32[64,512]{1,0:T(8,128)} %s0.1) | copy-start | bytes 393220
  12.9 10.3 %copy-start.4 = (s32[4]{0:T(128)S(1)}, s32[4]{0:T(128)}, u32[]{:S(2)}) copy-start(s32[4]{0:T(128)} %offsets_ref.1) | copy-start | bytes 52
  22.4 6.2 %collective-permute-start.4 = (f32[32,128]{1,0:T(8,128)S(1)}, f32[32,128]{1,0:T(8,128)S(1)}, u32[]{:S(2)}, u32[]{:S(2)}) collective-permute-start(f32[32,128]{1,0:T(8,128)S(1)} %get-tuple-element.19.send_ref), channel_id=1, source_target_pairs={{0,252},{4,8},{8,4},{12,16},{16,12},{20,24},{24,20},{28,32},{32,28... | collective-permute-start | bytes 49160 | tf_op jit(solution)/shard_map/ppermute | solution.py:349
  23.2 8.2 %copy-start = (f32[32]{0:T(128)S(1)}, f32[32]{0:T(128)}, u32[]{:S(2)}) copy-start(f32[32]{0:T(128)} %param.16) | copy-start | bytes 388
  23.2 8.1 %copy-start.1 = (f32[32]{0:T(128)S(1)}, f32[32]{0:T(128)}, u32[]{:S(2)}) copy-start(f32[32]{0:T(128)} %param.17) | copy-start | bytes 388
  28.5 2.8 %collective-permute-start.5 = (f32[64,1152]{1,0:T(8,128)S(1)}, f32[64,1152]{1,0:T(8,128)S(1)}, u32[]{:S(2)}, u32[]{:S(2)}) collective-permute-start(f32[64,1152]{1,0:T(8,128)S(1)} %get-tuple-element.22), channel_id=1, source_target_pairs={{0,4},{4,0},{8,12},{12,8},{16,20},{20,16},{24,28},{28,24},{32,36},... | collective-permute-start | bytes 884744 | tf_op jit(solution)/shard_map/ppermute | solution.py:21
  31.6 4.1 %collective-permute-start.6 = (f32[16,1536]{1,0:T(8,128)S(1)}, f32[16,1536]{1,0:T(8,128)S(1)}, u32[]{:S(2)}, u32[]{:S(2)}) collective-permute-start(f32[16,1536]{1,0:T(8,128)S(1)} %get-tuple-element.27), channel_id=1, source_target_pairs={{0,1},{1,0},{2,3},{3,2},{4,5},{5,4},{6,7},{7,6},{8,9},{9,8},{10,11... | collective-permute-start | bytes 294920 | tf_op jit(solution)/shard_map/ppermute | solution.py:21
  33.0 7.3 %collective-permute-start.7 = (f32[16,1536]{1,0:T(8,128)S(1)}, f32[16,1536]{1,0:T(8,128)S(1)}, u32[]{:S(2)}, u32[]{:S(2)}) collective-permute-start(f32[16,1536]{1,0:T(8,128)S(1)} %get-tuple-element.28), channel_id=1, source_target_pairs={{0,2},{1,3},{2,0},{3,1},{4,6},{5,7},{6,4},{7,5},{8,10},{9,11},{10,... | collective-permute-start | bytes 294920 | tf_op jit(solution)/shard_map/ppermute | solution.py:21
  35.6 7.2 %collective-permute-start.8 = (f32[16,1536]{1,0:T(8,128)S(1)}, f32[16,1536]{1,0:T(8,128)S(1)}, u32[]{:S(2)}, u32[]{:S(2)}) collective-permute-start(f32[16,1536]{1,0:T(8,128)S(1)} %get-tuple-element.29), channel_id=1, source_target_pairs={{0,3},{1,2},{2,1},{3,0},{4,7},{5,6},{6,5},{7,4},{8,11},{9,10},{10,... | collective-permute-start | bytes 294920 | tf_op jit(solution)/shard_map/ppermute | solution.py:21
  42.9 6.5 %collective-permute-start.10 = (f32[16,512]{1,0:T(8,128)S(1)}, f32[16,512]{1,0:T(8,128)S(1)}, u32[]{:S(2)}, u32[]{:S(2)}) collective-permute-start(f32[16,512]{1,0:T(8,128)S(1)} %get-tuple-element.32), channel_id=1, source_target_pairs={{0,16},{4,20},{8,24},{12,28},{16,32},{20,36},{24,40},{28,44},{32,4... | collective-permute-start | bytes 98312 | tf_op jit(solution)/shard_map/ppermute | solution.py:17
  43.7 6.1 %collective-permute-start.9 = (f32[16,512]{1,0:T(8,128)S(1)}, f32[16,512]{1,0:T(8,128)S(1)}, u32[]{:S(2)}, u32[]{:S(2)}) collective-permute-start(f32[16,512]{1,0:T(8,128)S(1)} %get-tuple-element.31), channel_id=1, source_target_pairs={{0,8},{4,12},{8,16},{12,20},{16,24},{20,28},{24,32},{28,36},{32,40... | collective-permute-start | bytes 98312 | tf_op jit(solution)/shard_map/ppermute | solution.py:17

commit v3 on v2

--- a/solution.py
+++ b/solution.py
@@ -52,8 +52,8 @@
     return jnp.where(even, second[0] + pltpu.roll(second[0], 7, 0), second[1] + pltpu.roll(second[1], 1, 0))
 
 
-def conv_kernel(w_ref, bias_ref, ow_ref, *refs):
-    x_refs, (prior_ref, own_ref, send_ref, t_ref, a_ref, b_ref) = refs[:-6], refs[-6:]
+def conv_kernel(counts_ref, w_ref, bias_ref, ow_ref, *refs):
+    x_refs, (prior_ref, own_ref, send_ref, live_ref, t_ref, a_ref, b_ref) = refs[:-7], refs[-7:]
     step = pl.program_id(0)
     channels = w_ref.shape[1]
     cols = prior_ref.shape[1]
@@ -71,14 +71,15 @@
             t_ref[j * taps : (j + 1) * taps, :channels] = even
             t_ref[j * taps : (j + 1) * taps, channels:] = odd
         b_ref[pairs - 1] = jnp.zeros(b_ref.shape[1:], F32)
+        live_ref[...] = jnp.broadcast_to(counts_ref[...], live_ref.shape)
         own_ref[...] = jnp.zeros_like(own_ref)
         send_ref[...] = jnp.zeros_like(send_ref)
 
-    bias = column(jnp.concatenate([bias_ref[...]] * 2, axis=1))
-    half_weight = column(jnp.concatenate([ow_ref[...]] * 2, axis=1)) * 0.5
-    lane = lane_index((2 * outs, LANES))
+    bias = column(jnp.concatenate([bias_ref[...]] * 4, axis=1))
+    half_weight = column(jnp.concatenate([ow_ref[...]] * 4, axis=1)) * 0.5
+    lane = lane_index((4 * outs, LANES))
     col = lane_index((block, cols))
-    inner = jnp.logical_and(col > 0, col < cols - 1)
+    middle = jnp.logical_and(col > 0, col < cols - 1)
 
     def load(half):
         parts = [jnp.swapaxes(x[:, half * block : (half + 1) * block, :], 0, 1) for x in x_refs]
@@ -88,21 +89,27 @@
         both = x[2 * pair : 2 * pair + 2].reshape(2 * channels, cols)
         p_ref[pair] = jnp.dot(t_ref[...], both, preferred_element_type=F32)
 
-    def two_rows(batch, *terms):
+    def add_rows(batch, *groups):
         sums, edges = batch
-        both = sum(p_ref[pair, j * taps : (j + 2) * taps, :] for p_ref, pair, j in terms)
+        both = [sum(p_ref[pair, j * taps : (j + 2) * taps, :] for p_ref, pair, j in terms) for terms in groups]
 
         def tap(b):
-            return jnp.concatenate([both[n * taps + b * outs : n * taps + (b + 1) * outs] for n in range(2)], axis=0)
+            return jnp.concatenate(
+                [part[n * taps + b * outs : n * taps + (b + 1) * outs] for part in both for n in range(2)], axis=0
+            )
 
         tail = cols - LANES
+        count = 2 * len(groups)
         before = pltpu.roll(tap(0), 1, 1)
         after = pltpu.roll(tap(2), cols - 1, 1)
         here = tap(1)
-        score = weighted_silu(before + here + after + bias, half_weight)
-        own = jnp.where(lane == 0, here[:, :LANES] + after[:, :LANES], here[:, tail:] + before[:, tail:])
-        send = jnp.where(lane == 0, before[:, :LANES], after[:, tail:])
-        for n in range(2):
+        score = weighted_silu(
+            before + here + after + bias[: count * outs], half_weight[: count * outs]
+        )
+        first = lane[: count * outs] == 0
+        own = jnp.where(first, here[:, :LANES] + after[:, :LANES], here[:, tail:] + before[:, tail:])
+        send = jnp.where(first, before[:, :LANES], after[:, tail:])
+        for n in range(count):
             i = len(sums)
             cut = slice(n * outs, (n + 1) * outs)
             sums.append(sum(score[n * outs + k : n * outs + k + 8] for k in range(0, outs, 8)))
@@ -115,24 +122,25 @@
 
     def store(batch, base):
         sums, edges = batch
-        prior_ref[pl.ds(pl.multiple_of(base, block), block), :] = jnp.where(inner, gather_rows(sums), 0.0)
+        prior_ref[pl.ds(pl.multiple_of(base, block), block), :] = jnp.where(middle, gather_rows(sums), 0.0)
         row = base - (block - 1) + (lane[:outs] >> 1)
         valid = jnp.logical_and(row >= 0, row < strip_rows)
         turn = (2 * base + LANES - 2 * (block - 1)) % LANES
         for ref, ends in zip((own_ref, send_ref), edges):
             ref[...] += pltpu.roll(jnp.where(valid, ends, 0.0), turn, 1)
 
-    def inner_rows(batch, p_ref, pair):
-        two_rows(batch, (p_ref, pair, 2), (p_ref, pair + 1, 0))
+    def inner(p_ref, pair):
+        return ((p_ref, pair, 2), (p_ref, pair + 1, 0))
 
     def phase(p_ref, earlier_ref, half, base):
         x = load(half)
         batch = new_batch()
-        for pair in range(pairs):
-            multiply(p_ref, x, pair)
-            if pair < pairs - 1:
-                inner_rows(batch, earlier_ref, pair)
-        two_rows(batch, (earlier_ref, pairs - 1, 2), (p_ref, 0, 0))
+        multiply(p_ref, x, 0)
+        multiply(p_ref, x, 1)
+        add_rows(batch, inner(earlier_ref, 0), inner(earlier_ref, 1))
+        multiply(p_ref, x, 2)
+        multiply(p_ref, x, 3)
+        add_rows(batch, inner(earlier_ref, 2), ((earlier_ref, pairs - 1, 2), (p_ref, 0, 0)))
         store(batch, base)
 
     start = step * 2 * block
@@ -142,9 +150,8 @@
     @pl.when(step == pl.num_programs(0) - 1)
     def _():
         batch = new_batch()
-        for pair in range(pairs - 1):
-            inner_rows(batch, b_ref, pair)
-        two_rows(batch, (b_ref, pairs - 1, 2))
+        add_rows(batch, inner(b_ref, 0), inner(b_ref, 1))
+        add_rows(batch, inner(b_ref, 2), ((b_ref, pairs - 1, 2),))
         store(batch, strip_rows)
 
 
@@ -152,7 +159,7 @@
     return pltpu.with_memory_space_constraint(x, pltpu.HBM)
 
 
-def conv_prior(features, weight, bias, out_weight):
+def conv_prior(counts, features, weight, bias, out_weight):
     channels, strip_rows, cols = features.shape
     outs = bias.shape[0]
     block = 8
@@ -163,16 +170,17 @@
     return pl.pallas_call(
         conv_kernel,
         grid=(strip_rows // (2 * block),),
-        in_specs=[full((9 * outs, channels)), full((1, outs)), full((1, outs))]
+        in_specs=[full((1, 1)), full((9 * outs, channels)), full((1, outs)), full((1, outs))]
         + [
             pl.BlockSpec((channels // cuts, 2 * block, cols), functools.partial(lambda n, i: (n, i, 0), n))
             for n in range(cuts)
         ],
-        out_specs=[full((strip_rows + block, cols)), full((outs, LANES)), full((outs, LANES))],
+        out_specs=[full((strip_rows + block, cols)), full((outs, LANES)), full((outs, LANES)), full((8, LANES))],
         out_shape=[
             jax.ShapeDtypeStruct((strip_rows + block, cols), F32),
             jax.ShapeDtypeStruct((outs, LANES), F32),
             jax.ShapeDtypeStruct((outs, LANES), F32),
+            jax.ShapeDtypeStruct((8, LANES), jnp.int32),
         ],
         scratch_shapes=[
             pltpu.VMEM((4 * taps, 2 * channels), BF16),
@@ -181,7 +189,7 @@
         ],
         compiler_params=pltpu.CompilerParams(vmem_limit_bytes=32 << 20),
         cost_estimate=pl.CostEstimate(flops=8_000_000_000, bytes_accessed=9_000_000, transcendentals=1_000_000),
-    )(*[far(x) for x in (flat, bias.reshape(1, outs), out_weight.reshape(1, outs))], *([far(features)] * cuts))
+    )(counts.reshape(1, 1), *[far(x) for x in (flat, bias.reshape(1, outs), out_weight.reshape(1, outs))], *([far(features)] * cuts))
 
 
 def split(x):
@@ -189,17 +197,29 @@
     return high, (x - high.astype(F32)).astype(BF16)
 
 
+HALF = 32
+
+
+def pair_rows(which):
+    mine = lax.axis_index("grp") // 2
+    return pl.multiple_of((mine if which else 1 - mine) * HALF, HALF)
+
+
 def exposure_kernel(
-    offsets_ref, counts_ref, s0, s1, s2, s3, s4, record_ref, taps_ref, send_ref, keep_ref, give_ref, ext_ref, acc_ref
+    halves, offsets_ref, counts_ref, s0, s1, s2, s3, s4, record_ref, taps_ref, send_ref, *refs
 ):
-    slots, rows, width = record_ref.shape
+    outs, (ext_ref, acc_ref) = refs[:-2], refs[-2:]
+    slots, _, width = record_ref.shape
+    rows = HALF * len(halves)
+    tops = [pl.ds(pair_rows(which), HALF) for which in halves]
     cols = s0.shape[1]
-    tap_count = taps_ref.shape[2]
+    tap_count = taps_ref.shape[1]
     pieces = width // tap_count
     tiles = width // LANES
     per = tap_count // LANES
     for d, part in enumerate((s0, s1, s2, s3, s4)):
-        ext_ref[:, d * cols : (d + 1) * cols] = part[...]
+        for h, top in enumerate(tops):
+            ext_ref[h * HALF : (h + 1) * HALF, d * cols : (d + 1) * cols] = part[top, :]
     acc_ref[...] = jnp.zeros_like(acc_ref)
 
     def add_slot(n):
@@ -208,7 +228,7 @@
         base = pl.multiple_of(offset - rest, LANES)
         lane = lane_index((rows, LANES))
 
-        taps = taps_ref[n]
+        taps = taps_ref[n : n + 1, :]
         wide = jnp.concatenate([taps, jnp.zeros_like(taps)], axis=1)
         band = pltpu.roll(jnp.broadcast_to(wide, (tap_count, 2 * tap_count)), 0, 1, stride=1, stride_axis=0)
         first, second = split(band[:, :tap_count]), split(band[:, tap_count:])
@@ -234,9 +254,9 @@
             [jnp.concatenate(window[p * per : (p + 1) * per], axis=1) for p in range(pieces)], axis=0
         )
         record = jnp.concatenate(
-            [record_ref[n, :, p * tap_count : (p + 1) * tap_count] for p in range(pieces)], axis=0
+            [record_ref[n, top, p * tap_count : (p + 1) * tap_count] for p in range(pieces) for top in tops], axis=0
         )
-        live = jnp.where(counts_ref[...] > n, 1.0, 0.0)
+        live = jnp.where(counts_ref[:1, :1] > n, 1.0, 0.0)
         residual = (record - banded(stacked, pieces - 1, 0)) * live
         back = banded(residual, 1, 1)
         moved = []
@@ -253,43 +273,44 @@
     for n in range(slots):
         add_slot(n)
 
-    for d in range(5):
-        to_ref = give_ref if d % 2 else keep_ref
-        to_ref[:, d // 2 * cols : (d // 2 + 1) * cols] = acc_ref[:, d * cols : (d + 1) * cols]
-    outs = send_ref.shape[0]
-    give_ref[:outs, 2 * cols :] = send_ref[...]
-    give_ref[outs:, 2 * cols :] = jnp.zeros((rows - outs, LANES), F32)
-
-
-def exposure_terms(offsets, counts, sky_parts, exposures, psf_taps, send):
-    slots, rows, width = exposures.shape
+    for h, which in enumerate(halves):
+        band = slice(h * HALF, (h + 1) * HALF)
+        keep_ref, give_ref = outs[2 * h : 2 * h + 2]
+        for d in range(5):
+            to_ref = give_ref if d % 2 else keep_ref
+            to_ref[:, d // 2 * cols : (d // 2 + 1) * cols] = acc_ref[band, d * cols : (d + 1) * cols]
+        if not which:
+            give_ref[:, 2 * cols :] = send_ref[...]
+
+
+def exposure_terms(halves, offsets, counts, sky_parts, exposures, psf_taps, send):
     cols = sky_parts[0].shape[1]
     reach = len(sky_parts) * cols
-    keep = (rows, 3 * cols)
-    give = (rows, 2 * cols + LANES)
+    shapes = []
+    for which in halves:
+        shapes += [(HALF, 3 * cols), (HALF, 2 * cols + (0 if which else LANES))]
     near = pl.BlockSpec(memory_space=pltpu.VMEM)
     few = pl.BlockSpec(memory_space=pltpu.SMEM)
     return pl.pallas_call(
-        exposure_kernel,
+        functools.partial(exposure_kernel, halves),
         in_specs=[few] + [near] * (len(sky_parts) + 4),
-        out_specs=[near] * 2,
-        out_shape=[jax.ShapeDtypeStruct(keep, F32), jax.ShapeDtypeStruct(give, F32)],
-        scratch_shapes=[pltpu.VMEM((rows, reach), F32), pltpu.VMEM((rows, reach), F32)],
+        out_specs=[near] * len(shapes),
+        out_shape=[jax.ShapeDtypeStruct(shape, F32) for shape in shapes],
+        scratch_shapes=[pltpu.VMEM((HALF * len(halves), reach), F32)] * 2,
         compiler_params=pltpu.CompilerParams(vmem_limit_bytes=32 << 20),
-        cost_estimate=pl.CostEstimate(flops=6_000_000_000, bytes_accessed=4_000_000, transcendentals=0),
-    )(offsets, counts.reshape(1, 1), *sky_parts, exposures, psf_taps.reshape(slots, 1, -1), send)
-
-
-def join_kernel(keep_ref, got_ref, cross_ref, prior_ref, own_ref, bias_ref, ow_ref, *outs):
-    outs, full_ref = outs[:-1], outs[-1]
+        cost_estimate=pl.CostEstimate(flops=3_000_000_000 * len(halves), bytes_accessed=2_000_000, transcendentals=0),
+    )(offsets, counts, *sky_parts, exposures, psf_taps, send)
+
+
+def join_kernel(which, keep_ref, got_ref, beside_ref, cross_ref, prior_ref, own_ref, bias_ref, ow_ref, out0, out1, full_ref):
     second = lax.axis_index("sky") % 2 == 1
-    group = lax.axis_index("grp")
-    share, width = outs[0].shape
+    low_half = lax.axis_index("grp") % 2
+    share, width = out0.shape
     cols = width // 3
-    rows = keep_ref.shape[0]
+    rows = full_ref.shape[0]
     channels = own_ref.shape[0]
     lane = lane_index((channels, LANES))
-    beside = got_ref[:channels, 2 * cols :]
+    beside = beside_ref[:, 2 * cols :]
     from_beside = jnp.logical_xor((lane & 1) == 0, second)
     edge = own_ref[...] + jnp.where(from_beside, beside, cross_ref[...]) + column(bias_ref[...])
     score = jnp.sum(weighted_silu(edge, column(ow_ref[...]) * 0.5), axis=0, keepdims=True)
@@ -300,16 +321,17 @@
     col = lane_index((rows, cols))
     skipped = prior_ref.shape[0] - rows - 1
     full_ref[...] = (
-        keep_ref[:, :cols]
-        + prior_ref[skipped : skipped + rows, :]
+        prior_ref[skipped : skipped + rows, :]
         + jnp.where(col == 0, first, 0.0)
         + jnp.where(col == cols - 1, last, 0.0)
     )
-    for k, out in enumerate(outs):
-        top = pl.ds(pl.multiple_of((group ^ k) * share, share), share)
+    for k, out in enumerate((out0, out1)):
+        start = pl.multiple_of((low_half ^ k) * share, share)
+        top = pl.ds(start, share)
         low = got_ref[top, :cols]
         high = got_ref[top, cols : 2 * cols]
-        out[:, :cols] = full_ref[top, :] + jnp.where(second, low, 0.0)
+        prior = full_ref[pl.ds(pl.multiple_of(pair_rows(which) + start, share), share), :]
+        out[:, :cols] = keep_ref[top, :cols] + prior + jnp.where(second, low, 0.0)
         out[:, cols : 2 * cols] = keep_ref[top, cols : 2 * cols] + jnp.where(second, high, low)
         out[:, 2 * cols :] = keep_ref[top, 2 * cols :] + jnp.where(second, 0.0, high)
 
@@ -344,19 +366,29 @@
     parts = [sky_strip]
     for distance in range(1, reach_blocks + 1):
         parts.append(shifted(sky_strip, "sky", -distance))
-    prior, own_edge, send = conv_prior(features, conv_weight, conv_bias, out_weight)
+    prior, own_edge, send, live = conv_prior(counts, features, conv_weight, conv_bias, out_weight)
     n_sky = lax.axis_size("sky")
     cross = lax.ppermute(send, "sky", [(i, (i - 1 if i % 2 == 0 else i + 1) % n_sky) for i in range(n_sky)])
-    keep, give = exposure_terms(offsets, counts, parts, exposures, psf_taps, send)
-    give, cross = lax.optimization_barrier((give, cross))
-    got = partner(give, "sky", 1)
-    terms = small_call(
-        join_kernel, [(share, 3 * cols)] * n_grp, keep, got, cross, prior, own_edge,
-        conv_bias.reshape(1, -1), out_weight.reshape(1, -1), scratch=[(strip_rows, cols)],
-    )
-    received = [terms[0]] + [partner(terms[k], "grp", k) for k in range(1, n_grp)]
-    own, near, far = small_call(sum_kernel, [(share, cols)] * 3, *received)
-    return own + shifted(near, "sky", 2) + shifted(far, "sky", 4)
+    keep_a, give_a = exposure_terms((0,), offsets, live, parts, exposures, psf_taps, send)
+    keep_b, give_b = exposure_terms((1,), offsets, live, parts, exposures, psf_taps, send)
+    got_a = partner(give_a, "sky", 1)
+    edges = (cross, prior, own_edge, conv_bias.reshape(1, -1), out_weight.reshape(1, -1))
+
+    def join(which, keep, got):
+        return small_call(
+            functools.partial(join_kernel, which), [(share, 3 * cols)] * 2, keep, got, got_a, *edges,
+            scratch=[(strip_rows, cols)],
+        )
+
+    to_2, to_3 = join(0, keep_a, got_a)
+    from_2, from_3 = partner(to_2, "grp", 2), partner(to_3, "grp", 3)
+    give_b, to_2 = lax.optimization_barrier((give_b, to_2))
+    got_b = partner(give_b, "sky", 1)
+    kept, to_1 = join(1, keep_b, got_b)
+    received = [kept, partner(to_1, "grp", 1), from_2, from_3]
+    own, near, distant = small_call(sum_kernel, [(share, cols)] * 3, *received)
+    distant = shifted(distant, "sky", 4)
+    return own + shifted(near, "sky", 2) + distant
 
 
 def solution(mesh):

time: 50.4 us -> 47.8 us (0.948); the launches traced: 50.4 us -> 46.9 us
  waiting for transfers between devices: 12.1 us -> 7.29 us
  Pallas kernels: 15 us -> 16 us
    ppermute x4 -> x5, waiting for transfers between devices: 8.44 us -> 3.64 us  [partner(): lax.ppermute(x, axis, [(i, i ^ mask) for i in range(lax.axis_size(axis))])]
    pallas_call x1 -> x2, Pallas kernels: 5.28 us -> 6.29 us  [exposure_terms(): pl.pallas_call(functools.partial(exposure_kernel, halves), in_specs=[few]...]
    ppermute x4 -> x5, starting transfers between devices: 5.63 us -> 5.59 us  [partner(): lax.ppermute(x, axis, [(i, i ^ mask) for i in range(lax.axis_size(axis))])]
  transfers between devices with their start and end apart: 11 -> 12, of which waited for: 6 -> 4; matrix products, arithmetic and copies ran while one was open for 0% -> 0% of each run, Pallas kernels for 29% -> 34%
where the time goes in v3:
time: 47.8 us; the launch traced here: 46.9 us
  starting transfers between devices  22.1 us (46%)
  Pallas kernels  16 us (33%)
  waiting for transfers between devices  7.29 us (15%)
  between operations  0.85 us (2%)
  other arithmetic  0.62 us (1%)
    ppermute x6, starting transfers between devices, shifted(): lax.ppermute(x, axis, [(i, (i + by) % length) for i in range(length)])  16.4 us
    pallas_call x1, Pallas kernels, conv_prior(): pl.pallas_call(conv_kernel, grid=(strip_rows // (2 * block),), in_specs=[...  9.32 us
    pallas_call x2, Pallas kernels, exposure_terms(): pl.pallas_call(functools.partial(exposure_kernel, halves), in_specs=[few]...  6.29 us
    ppermute x5, starting transfers between devices, partner(): lax.ppermute(x, axis, [(i, i ^ mask) for i in range(lax.axis_size(axis))])  5.59 us
    ppermute x6, waiting for transfers between devices, shifted(): lax.ppermute(x, axis, [(i, (i + by) % length) for i in range(length)])  3.65 us
    ppermute x5, waiting for transfers between devices, partner(): lax.ppermute(x, axis, [(i, i ^ mask) for i in range(lax.axis_size(axis))])  3.64 us
  transfers between devices with their start and end apart: 12, of which 4 were waited for; matrix products, arithmetic and copies ran while one was open for 0% of the time, Pallas kernels for 34%

profile of v3, /device:TPU:1, one launch (start us, length us, event | category | flops | bytes accessed | tf_op | source)
XLA Modules:
  0.0 46.9 jit_solution(79030902793450815)
XLA Ops:
  0.0 3.2 %collective-permute-start = (f32[64,512]{1,0:T(8,128)}, f32[64,512]{1,0:T(8,128)S(1)}, u32[]{:S(2)}, u32[]{:S(2)}) collective-permute-start(f32[64,512]{1,0:T(8,128)} %s0.3), channel_id=1, source_target_pairs={{0,252},{4,0},{8,4},{12,8},{16,12},{20,16},{24,20},{28,24},{32,28}... | collective-permute-start | bytes 393224 | tf_op jit(solution)/shard_map/ppermute | solution.py:17
  3.2 6.0 %collective-permute-start.1 = (f32[64,512]{1,0:T(8,128)}, f32[64,512]{1,0:T(8,128)S(1)}, u32[]{:S(2)}, u32[]{:S(2)}) collective-permute-start(f32[64,512]{1,0:T(8,128)} %s0.3), channel_id=1, source_target_pairs={{0,248},{4,252},{8,0},{12,4},{16,8},{20,12},{24,16},{28,20},{32,24... | collective-permute-start | bytes 393224 | tf_op jit(solution)/shard_map/ppermute | solution.py:17
  9.3 0.7 %collective-permute-start.2 = (f32[64,512]{1,0:T(8,128)}, f32[64,512]{1,0:T(8,128)S(1)}, u32[]{:S(2)}, u32[]{:S(2)}) collective-permute-start(f32[64,512]{1,0:T(8,128)} %s0.3), channel_id=1, source_target_pairs={{0,244},{4,248},{8,252},{12,0},{16,4},{20,8},{24,12},{28,16},{32,2... | collective-permute-start | bytes 393224 | tf_op jit(solution)/shard_map/ppermute | solution.py:17
  10.0 2.9 %collective-permute-start.3 = (f32[64,512]{1,0:T(8,128)}, f32[64,512]{1,0:T(8,128)S(1)}, u32[]{:S(2)}, u32[]{:S(2)}) collective-permute-start(f32[64,512]{1,0:T(8,128)} %s0.3), channel_id=1, source_target_pairs={{0,240},{4,244},{8,248},{12,252},{16,0},{20,4},{24,8},{28,12},{32,... | collective-permute-start | bytes 393224 | tf_op jit(solution)/shard_map/ppermute | solution.py:17
  13.6 9.3 %shard_map.91 = (f32[72,512]{1,0:T(8,128)S(1)}, f32[32,128]{1,0:T(8,128)S(1)}, f32[32,128]{1,0:T(8,128)S(1)}, s32[8,128]{1,0:T(8,128)S(1)}) custom-call(s32[1,1]{1,0:T(1,128)} %bitcast.6.counts_ref, bf16[288,128]{1,0:T(8,128)(2,1)} %bitcast.13, f32[1,32]{1,0:T(1,128)} %bitcast.7, f32[1,32]{1,0:T(1,128)} %bitcast.10, bf16[128,64,512]{2,1,0:T(8,128)(2,1)} %refs_3_.1, ...), custom_call_target="tpu_custom_call" | custom-call | flops 8000000000 | bytes 9000000 | tf_op jit(solution)/shard_map/pallas_call | solution.py:170
  22.9 0.1 collective-permute-start.5
  23.1 0.0 copy-start
  23.1 0.0 copy-start.1
  23.1 3.1 %shard_map.93 = (f32[32,1536]{1,0:T(8,128)S(1)}, f32[32,1152]{1,0:T(8,128)S(1)}) custom-call(s32[4]{0:T(128)S(1)} %copy-done.5, s32[8,128]{1,0:T(8,128)S(1)} %get-tuple-element.21.counts_ref, f32[64,512]{1,0:T(8,128)S(1)} %copy-done.3, f32[64,512]{1,0:T(8,128)S(1)} %collective-permute-done.s1, f32[64,512]{1,0:T(8,128)S(1)} %collective-permute-done.1.s2, ...), custom_call_target="tpu_custom_call" | custom-call | flops 3000000000 | bytes 2000000 | tf_op jit(solution)/shard_map/pallas_call | solution.py:294
  26.2 1.6 %collective-permute-start.4 = (f32[32,1152]{1,0:T(8,128)S(1)}, f32[32,1152]{1,0:T(8,128)S(1)}, u32[]{:S(2)}, u32[]{:S(2)}) collective-permute-start(f32[32,1152]{1,0:T(8,128)S(1)} %get-tuple-element.26), channel_id=1, source_target_pairs={{0,4},{4,0},{8,12},{12,8},{16,20},{20,16},{24,28},{28,24},{32,36},... | collective-permute-start | bytes 442376 | tf_op jit(solution)/shard_map/ppermute | solution.py:21
  27.8 3.1 %shard_map.92 = (f32[32,1536]{1,0:T(8,128)S(1)}, f32[32,1024]{1,0:T(8,128)S(1)}) custom-call(s32[4]{0:T(128)S(1)} %copy-done.5, s32[8,128]{1,0:T(8,128)S(1)} %get-tuple-element.21.counts_ref, f32[64,512]{1,0:T(8,128)S(1)} %copy-done.3, f32[64,512]{1,0:T(8,128)S(1)} %collective-permute-done.s1, f32[64,512]{1,0:T(8,128)S(1)} %collective-permute-done.1.s2, ...), custom_call_target="tpu_custom_call" | custom-call | flops 3000000000 | bytes 2000000 | tf_op jit(solution)/shard_map/pallas_call | solution.py:294
  31.0 0.2 shard_map.94
  31.2 0.1 collective-permute-start.6
  31.4 3.0 %collective-permute-start.8 = (f32[16,1536]{1,0:T(8,128)S(1)}, f32[16,1536]{1,0:T(8,128)S(1)}, u32[]{:S(2)}, u32[]{:S(2)}) collective-permute-start(f32[16,1536]{1,0:T(8,128)S(1)} %get-tuple-element.29), channel_id=1, source_target_pairs={{0,2},{1,3},{2,0},{3,1},{4,6},{5,7},{6,4},{7,5},{8,10},{9,11},{10,... | collective-permute-start | bytes 294920 | tf_op jit(solution)/shard_map/ppermute | solution.py:21
  34.3 0.8 %collective-permute-start.9 = (f32[16,1536]{1,0:T(8,128)S(1)}, f32[16,1536]{1,0:T(8,128)S(1)}, u32[]{:S(2)}, u32[]{:S(2)}) collective-permute-start(f32[16,1536]{1,0:T(8,128)S(1)} %get-tuple-element.33), channel_id=1, source_target_pairs={{0,3},{1,2},{2,1},{3,0},{4,7},{5,6},{6,5},{7,4},{8,11},{9,10},{10,... | collective-permute-start | bytes 294920 | tf_op jit(solution)/shard_map/ppermute | solution.py:21
  35.1 0.2 shard_map.95
  35.3 0.1 collective-permute-start.7
  35.4 1.4 %collective-permute-done.8.c = f32[16,1536]{1,0:T(8,128)S(1)} collective-permute-done((f32[16,1536]{1,0:T(8,128)S(1)}, f32[16,1536]{1,0:T(8,128)S(1)}, u32[]{:S(2)}, u32[]{:S(2)}) %collective-permute-start.8) | collective-permute-done | bytes 98336 | tf_op jit(solution)/shard_map/ppermute | solution.py:21
  36.9 2.2 %collective-permute-done.9.d = f32[16,1536]{1,0:T(8,128)S(1)} collective-permute-done((f32[16,1536]{1,0:T(8,128)S(1)}, f32[16,1536]{1,0:T(8,128)S(1)}, u32[]{:S(2)}, u32[]{:S(2)}) %collective-permute-start.9) | collective-permute-done | bytes 98336 | tf_op jit(solution)/shard_map/ppermute | solution.py:21
  39.1 1.1 %collective-permute-start.11 = (f32[16,512]{1,0:T(8,128)S(1)}, f32[16,512]{1,0:T(8,128)S(1)}, u32[]{:S(2)}, u32[]{:S(2)}) collective-permute-start(f32[16,512]{1,0:T(8,128)S(1)} %get-tuple-element.36), channel_id=1, source_target_pairs={{0,16},{4,20},{8,24},{12,28},{16,32},{20,36},{24,40},{28,44},{32,4... | collective-permute-start | bytes 98312 | tf_op jit(solution)/shard_map/ppermute | solution.py:17
  40.2 2.4 %collective-permute-start.10 = (f32[16,512]{1,0:T(8,128)S(1)}, f32[16,512]{1,0:T(8,128)S(1)}, u32[]{:S(2)}, u32[]{:S(2)}) collective-permute-start(f32[16,512]{1,0:T(8,128)S(1)} %get-tuple-element.35), channel_id=1, source_target_pairs={{0,8},{4,12},{8,16},{12,20},{16,24},{20,28},{24,32},{28,36},{32,40... | collective-permute-start | bytes 98312 | tf_op jit(solution)/shard_map/ppermute | solution.py:17
  42.7 2.9 %collective-permute-done.11 = f32[16,512]{1,0:T(8,128)S(1)} collective-permute-done((f32[16,512]{1,0:T(8,128)S(1)}, f32[16,512]{1,0:T(8,128)S(1)}, u32[]{:S(2)}, u32[]{:S(2)}) %collective-permute-start.11) | collective-permute-done | bytes 32800 | tf_op jit(solution)/shard_map/ppermute | solution.py:17
  45.6 0.7 %collective-permute-done.10 = f32[16,512]{1,0:T(8,128)S(1)} collective-permute-done((f32[16,512]{1,0:T(8,128)S(1)}, f32[16,512]{1,0:T(8,128)S(1)}, u32[]{:S(2)}, u32[]{:S(2)}) %collective-permute-start.10) | collective-permute-done | bytes 32800 | tf_op jit(solution)/shard_map/ppermute | solution.py:17
  46.3 0.6 %add_add_fusion = f32[16,512]{1,0:T(8,128)} fusion(f32[16,512]{1,0:T(8,128)S(1)} %collective-permute-done.11, f32[16,512]{1,0:T(8,128)S(1)} %get-tuple-element.34, f32[16,512]{1,0:T(8,128)S(1)} %collective-permute-done.10), kind=kLoop, calls=%fused_computation | loop fusion | flops 16384 | bytes 131072 | tf_op jit(solution)/shard_map/add | solution.py:391
  (19 shorter events, 0.1 us)
Async XLA Ops:
  0.0 23.0 %collective-permute-start = (f32[64,512]{1,0:T(8,128)}, f32[64,512]{1,0:T(8,128)S(1)}, u32[]{:S(2)}, u32[]{:S(2)}) collective-permute-start(f32[64,512]{1,0:T(8,128)} %s0.3), channel_id=1, source_target_pairs={{0,252},{4,0},{8,4},{12,8},{16,12},{20,16},{24,20},{28,24},{32,28}... | collective-permute-start | bytes 393224 | tf_op jit(solution)/shard_map/ppermute | solution.py:17
  3.2 19.7 %collective-permute-start.1 = (f32[64,512]{1,0:T(8,128)}, f32[64,512]{1,0:T(8,128)S(1)}, u32[]{:S(2)}, u32[]{:S(2)}) collective-permute-start(f32[64,512]{1,0:T(8,128)} %s0.3), channel_id=1, source_target_pairs={{0,248},{4,252},{8,0},{12,4},{16,8},{20,12},{24,16},{28,20},{32,24... | collective-permute-start | bytes 393224 | tf_op jit(solution)/shard_map/ppermute | solution.py:17
  9.3 13.7 %collective-permute-start.2 = (f32[64,512]{1,0:T(8,128)}, f32[64,512]{1,0:T(8,128)S(1)}, u32[]{:S(2)}, u32[]{:S(2)}) collective-permute-start(f32[64,512]{1,0:T(8,128)} %s0.3), channel_id=1, source_target_pairs={{0,244},{4,248},{8,252},{12,0},{16,4},{20,8},{24,12},{28,16},{32,2... | collective-permute-start | bytes 393224 | tf_op jit(solution)/shard_map/ppermute | solution.py:17
  10.0 13.0 %collective-permute-start.3 = (f32[64,512]{1,0:T(8,128)}, f32[64,512]{1,0:T(8,128)S(1)}, u32[]{:S(2)}, u32[]{:S(2)}) collective-permute-start(f32[64,512]{1,0:T(8,128)} %s0.3), channel_id=1, source_target_pairs={{0,240},{4,244},{8,248},{12,252},{16,0},{20,4},{24,8},{28,12},{32,... | collective-permute-start | bytes 393224 | tf_op jit(solution)/shard_map/ppermute | solution.py:17
  13.5 9.5 %copy-start.2 = (f32[4,64,2048]{2,1,0:T(8,128)S(1)}, f32[4,64,2048]{2,1,0:T(8,128)}, u32[]{:S(2)}) copy-start(f32[4,64,2048]{2,1,0:T(8,128)} %record_ref.3) | copy-start | bytes 6291460
  13.5 9.5 %copy-start.3 = (f32[64,512]{1,0:T(8,128)S(1)}, f32[64,512]{1,0:T(8,128)}, u32[]{:S(2)}) copy-start(f32[64,512]{1,0:T(8,128)} %s0.3) | copy-start | bytes 393220
  13.5 9.5 %copy-start.4 = (f32[4,256]{1,0:T(4,128)S(1)}, f32[4,256]{1,0:T(4,128)}, u32[]{:S(2)}) copy-start(f32[4,256]{1,0:T(4,128)} %taps_ref.3) | copy-start | bytes 12292
  13.5 9.5 %copy-start.5 = (s32[4]{0:T(128)S(1)}, s32[4]{0:T(128)}, u32[]{:S(2)}) copy-start(s32[4]{0:T(128)} %offsets_ref.3) | copy-start | bytes 52
  22.9 8.1 %collective-permute-start.5 = (f32[32,128]{1,0:T(8,128)S(1)}, f32[32,128]{1,0:T(8,128)S(1)}, u32[]{:S(2)}, u32[]{:S(2)}) collective-permute-start(f32[32,128]{1,0:T(8,128)S(1)} %get-tuple-element.22.send_ref), channel_id=1, source_target_pairs={{0,252},{4,8},{8,4},{12,16},{16,12},{20,24},{24,20},{28,32},{32,28... | collective-permute-start | bytes 49160 | tf_op jit(solution)/shard_map/ppermute | solution.py:371
  23.1 8.0 %copy-start = (f32[32]{0:T(128)S(1)}, f32[32]{0:T(128)}, u32[]{:S(2)}) copy-start(f32[32]{0:T(128)} %param.16) | copy-start | bytes 388
  23.1 7.9 %copy-start.1 = (f32[32]{0:T(128)S(1)}, f32[32]{0:T(128)}, u32[]{:S(2)}) copy-start(f32[32]{0:T(128)} %param.17) | copy-start | bytes 388
  26.2 4.8 %collective-permute-start.4 = (f32[32,1152]{1,0:T(8,128)S(1)}, f32[32,1152]{1,0:T(8,128)S(1)}, u32[]{:S(2)}, u32[]{:S(2)}) collective-permute-start(f32[32,1152]{1,0:T(8,128)S(1)} %get-tuple-element.26), channel_id=1, source_target_pairs={{0,4},{4,0},{8,12},{12,8},{16,20},{20,16},{24,28},{28,24},{32,36},... | collective-permute-start | bytes 442376 | tf_op jit(solution)/shard_map/ppermute | solution.py:21
  31.2 3.9 %collective-permute-start.6 = (f32[32,1024]{1,0:T(8,128)S(1)}, f32[32,1024]{1,0:T(8,128)S(1)}, u32[]{:S(2)}, u32[]{:S(2)}) collective-permute-start(f32[32,1024]{1,0:T(8,128)S(1)} %get-tuple-element.30), channel_id=1, source_target_pairs={{0,4},{4,0},{8,12},{12,8},{16,20},{20,16},{24,28},{28,24},{32,36},... | collective-permute-start | bytes 393224 | tf_op jit(solution)/shard_map/ppermute | solution.py:21
  31.4 5.5 %collective-permute-start.8 = (f32[16,1536]{1,0:T(8,128)S(1)}, f32[16,1536]{1,0:T(8,128)S(1)}, u32[]{:S(2)}, u32[]{:S(2)}) collective-permute-start(f32[16,1536]{1,0:T(8,128)S(1)} %get-tuple-element.29), channel_id=1, source_target_pairs={{0,2},{1,3},{2,0},{3,1},{4,6},{5,7},{6,4},{7,5},{8,10},{9,11},{10,... | collective-permute-start | bytes 294920 | tf_op jit(solution)/shard_map/ppermute | solution.py:21
  34.3 4.7 %collective-permute-start.9 = (f32[16,1536]{1,0:T(8,128)S(1)}, f32[16,1536]{1,0:T(8,128)S(1)}, u32[]{:S(2)}, u32[]{:S(2)}) collective-permute-start(f32[16,1536]{1,0:T(8,128)S(1)} %get-tuple-element.33), channel_id=1, source_target_pairs={{0,3},{1,2},{2,1},{3,0},{4,7},{5,6},{6,5},{7,4},{8,11},{9,10},{10,... | collective-permute-start | bytes 294920 | tf_op jit(solution)/shard_map/ppermute | solution.py:21
  35.3 3.7 %collective-permute-start.7 = (f32[16,1536]{1,0:T(8,128)S(1)}, f32[16,1536]{1,0:T(8,128)S(1)}, u32[]{:S(2)}, u32[]{:S(2)}) collective-permute-start(f32[16,1536]{1,0:T(8,128)S(1)} %get-tuple-element.32), channel_id=1, source_target_pairs={{0,1},{1,0},{2,3},{3,2},{4,5},{5,4},{6,7},{7,6},{8,9},{9,8},{10,11... | collective-permute-start | bytes 294920 | tf_op jit(solution)/shard_map/ppermute | solution.py:21
  39.1 6.5 %collective-permute-start.11 = (f32[16,512]{1,0:T(8,128)S(1)}, f32[16,512]{1,0:T(8,128)S(1)}, u32[]{:S(2)}, u32[]{:S(2)}) collective-permute-start(f32[16,512]{1,0:T(8,128)S(1)} %get-tuple-element.36), channel_id=1, source_target_pairs={{0,16},{4,20},{8,24},{12,28},{16,32},{20,36},{24,40},{28,44},{32,4... | collective-permute-start | bytes 98312 | tf_op jit(solution)/shard_map/ppermute | solution.py:17
  40.2 6.1 %collective-permute-start.10 = (f32[16,512]{1,0:T(8,128)S(1)}, f32[16,512]{1,0:T(8,128)S(1)}, u32[]{:S(2)}, u32[]{:S(2)}) collective-permute-start(f32[16,512]{1,0:T(8,128)S(1)} %get-tuple-element.35), channel_id=1, source_target_pairs={{0,8},{4,12},{8,16},{12,20},{16,24},{20,28},{24,32},{28,36},{32,40... | collective-permute-start | bytes 98312 | tf_op jit(solution)/shard_map/ppermute | solution.py:17

commit v4 on v3

--- a/solution.py
+++ b/solution.py
@@ -53,7 +53,7 @@
 
 
 def conv_kernel(counts_ref, w_ref, bias_ref, ow_ref, *refs):
-    x_refs, (prior_ref, own_ref, send_ref, live_ref, t_ref, a_ref, b_ref) = refs[:-7], refs[-7:]
+    x_refs, (prior_ref, own_ref, send_ref, live_ref, t_ref, a_ref, b_ref, ends_ref) = refs[:-8], refs[-8:]
     step = pl.program_id(0)
     channels = w_ref.shape[1]
     cols = prior_ref.shape[1]
@@ -72,8 +72,6 @@
             t_ref[j * taps : (j + 1) * taps, channels:] = odd
         b_ref[pairs - 1] = jnp.zeros(b_ref.shape[1:], F32)
         live_ref[...] = jnp.broadcast_to(counts_ref[...], live_ref.shape)
-        own_ref[...] = jnp.zeros_like(own_ref)
-        send_ref[...] = jnp.zeros_like(send_ref)
 
     bias = column(jnp.concatenate([bias_ref[...]] * 4, axis=1))
     half_weight = column(jnp.concatenate([ow_ref[...]] * 4, axis=1)) * 0.5
@@ -89,8 +87,7 @@
         both = x[2 * pair : 2 * pair + 2].reshape(2 * channels, cols)
         p_ref[pair] = jnp.dot(t_ref[...], both, preferred_element_type=F32)
 
-    def add_rows(batch, *groups):
-        sums, edges = batch
+    def add_rows(sums, base, *groups):
         both = [sum(p_ref[pair, j * taps : (j + 2) * taps, :] for p_ref, pair, j in terms) for terms in groups]
 
         def tap(b):
@@ -113,35 +110,25 @@
             i = len(sums)
             cut = slice(n * outs, (n + 1) * outs)
             sums.append(sum(score[n * outs + k : n * outs + k + 8] for k in range(0, outs, 8)))
-            mine = (lane[cut] >> 1) == i
-            for m, ends in enumerate((own[cut], send[cut])):
-                edges[m] = jnp.where(mine, pltpu.roll(ends, 2 * i + 1, 1), edges[m])
-
-    def new_batch():
-        return [], [jnp.zeros((outs, LANES), F32)] * 2
-
-    def store(batch, base):
-        sums, edges = batch
+            ends_ref[0, base + i] = own[cut]
+            ends_ref[1, base + i] = send[cut]
+
+    def store(sums, base):
         prior_ref[pl.ds(pl.multiple_of(base, block), block), :] = jnp.where(middle, gather_rows(sums), 0.0)
-        row = base - (block - 1) + (lane[:outs] >> 1)
-        valid = jnp.logical_and(row >= 0, row < strip_rows)
-        turn = (2 * base + LANES - 2 * (block - 1)) % LANES
-        for ref, ends in zip((own_ref, send_ref), edges):
-            ref[...] += pltpu.roll(jnp.where(valid, ends, 0.0), turn, 1)
 
     def inner(p_ref, pair):
         return ((p_ref, pair, 2), (p_ref, pair + 1, 0))
 
     def phase(p_ref, earlier_ref, half, base):
         x = load(half)
-        batch = new_batch()
+        sums = []
         multiply(p_ref, x, 0)
         multiply(p_ref, x, 1)
-        add_rows(batch, inner(earlier_ref, 0), inner(earlier_ref, 1))
+        add_rows(sums, base, inner(earlier_ref, 0), inner(earlier_ref, 1))
         multiply(p_ref, x, 2)
         multiply(p_ref, x, 3)
-        add_rows(batch, inner(earlier_ref, 2), ((earlier_ref, pairs - 1, 2), (p_ref, 0, 0)))
-        store(batch, base)
+        add_rows(sums, base, inner(earlier_ref, 2), ((earlier_ref, pairs - 1, 2), (p_ref, 0, 0)))
+        store(sums, base)
 
     start = step * 2 * block
     phase(a_ref, b_ref, 0, start)
@@ -149,10 +136,16 @@
 
     @pl.when(step == pl.num_programs(0) - 1)
     def _():
-        batch = new_batch()
-        add_rows(batch, inner(b_ref, 0), inner(b_ref, 1))
-        add_rows(batch, inner(b_ref, 2), ((b_ref, pairs - 1, 2),))
-        store(batch, strip_rows)
+        sums = []
+        add_rows(sums, strip_rows, inner(b_ref, 0), inner(b_ref, 1))
+        add_rows(sums, strip_rows, inner(b_ref, 2), ((b_ref, pairs - 1, 2),))
+        store(sums, strip_rows)
+        spot = lane[:outs] >> 1
+        for m, ref in enumerate((own_ref, send_ref)):
+            total = jnp.zeros((outs, LANES), F32)
+            for row in range(strip_rows):
+                total = jnp.where(spot == row, pltpu.roll(ends_ref[m, row + block - 1], (2 * row + 1) % LANES, 1), total)
+            ref[...] = total
 
 
 def far(x):
@@ -186,6 +179,7 @@
             pltpu.VMEM((4 * taps, 2 * channels), BF16),
             pltpu.VMEM((block // 2, 4 * taps, cols), F32),
             pltpu.VMEM((block // 2, 4 * taps, cols), F32),
+            pltpu.VMEM((2, strip_rows + block, outs, LANES), F32),
         ],
         compiler_params=pltpu.CompilerParams(vmem_limit_bytes=32 << 20),
         cost_estimate=pl.CostEstimate(flops=8_000_000_000, bytes_accessed=9_000_000, transcendentals=1_000_000),
@@ -206,7 +200,7 @@
 
 
 def exposure_kernel(
-    halves, offsets_ref, counts_ref, s0, s1, s2, s3, s4, record_ref, taps_ref, send_ref, *refs
+    halves, offsets_ref, counts_ref, s0, s1, s4, s3, s2, record_ref, taps_ref, send_ref, *refs
 ):
     outs, (ext_ref, acc_ref) = refs[:-2], refs[-2:]
     slots, _, width = record_ref.shape
@@ -299,7 +293,7 @@
         scratch_shapes=[pltpu.VMEM((HALF * len(halves), reach), F32)] * 2,
         compiler_params=pltpu.CompilerParams(vmem_limit_bytes=32 << 20),
         cost_estimate=pl.CostEstimate(flops=3_000_000_000 * len(halves), bytes_accessed=2_000_000, transcendentals=0),
-    )(offsets, counts, *sky_parts, exposures, psf_taps, send)
+    )(offsets, counts, sky_parts[0], sky_parts[1], sky_parts[4], sky_parts[3], sky_parts[2], exposures, psf_taps, send)
 
 
 def join_kernel(which, keep_ref, got_ref, beside_ref, cross_ref, prior_ref, own_ref, bias_ref, ow_ref, out0, out1, full_ref):

time: 47.8 us -> 47.5 us (level)
  the two profiles are of different devices: /device:TPU:1 before, /device:TPU:8 now
where the time goes in v4:
time: 47.5 us; the launch traced here: 47.4 us
  starting transfers between devices  21.9 us (46%)
  Pallas kernels  15.8 us (33%)
  waiting for transfers between devices  8.28 us (17%)
  between operations  0.85 us (2%)
  other arithmetic  0.62 us (1%)
    ppermute x6, starting transfers between devices, shifted(): lax.ppermute(x, axis, [(i, (i + by) % length) for i in range(length)])  16.3 us
    pallas_call x1, Pallas kernels, conv_prior(): pl.pallas_call(conv_kernel, grid=(strip_rows // (2 * block),), in_specs=[...  9.07 us
    pallas_call x2, Pallas kernels, exposure_terms(): pl.pallas_call(functools.partial(exposure_kernel, halves), in_specs=[few]...  6.29 us
    ppermute x5, starting transfers between devices, partner(): lax.ppermute(x, axis, [(i, i ^ mask) for i in range(lax.axis_size(axis))])  5.45 us
    ppermute x6, waiting for transfers between devices, shifted(): lax.ppermute(x, axis, [(i, (i + by) % length) for i in range(length)])  4.53 us
    ppermute x5, waiting for transfers between devices, partner(): lax.ppermute(x, axis, [(i, i ^ mask) for i in range(lax.axis_size(axis))])  3.74 us
  transfers between devices with their start and end apart: 12, of which 5 were waited for; matrix products, arithmetic and copies ran while one was open for 0% of the time, Pallas kernels for 33%

profile of v4, /device:TPU:8, one launch (start us, length us, event | category | flops | bytes accessed | tf_op | source)
XLA Modules:
  0.0 47.4 jit_solution(17690869884370559798)
XLA Ops:
  0.0 7.5 %collective-permute-start = (f32[64,512]{1,0:T(8,128)}, f32[64,512]{1,0:T(8,128)S(1)}, u32[]{:S(2)}, u32[]{:S(2)}) collective-permute-start(f32[64,512]{1,0:T(8,128)} %s0.3), channel_id=1, source_target_pairs={{0,252},{4,0},{8,4},{12,8},{16,12},{20,16},{24,20},{28,24},{32,28}... | collective-permute-start | bytes 393224 | tf_op jit(solution)/shard_map/ppermute | solution.py:17
  7.5 0.8 %collective-permute-start.1 = (f32[64,512]{1,0:T(8,128)}, f32[64,512]{1,0:T(8,128)S(1)}, u32[]{:S(2)}, u32[]{:S(2)}) collective-permute-start(f32[64,512]{1,0:T(8,128)} %s0.3), channel_id=1, source_target_pairs={{0,240},{4,244},{8,248},{12,252},{16,0},{20,4},{24,8},{28,12},{32,... | collective-permute-start | bytes 393224 | tf_op jit(solution)/shard_map/ppermute | solution.py:17
  8.3 0.3 collective-permute-start.2
  8.7 3.2 %collective-permute-start.3 = (f32[64,512]{1,0:T(8,128)}, f32[64,512]{1,0:T(8,128)S(1)}, u32[]{:S(2)}, u32[]{:S(2)}) collective-permute-start(f32[64,512]{1,0:T(8,128)} %s0.3), channel_id=1, source_target_pairs={{0,248},{4,252},{8,0},{12,4},{16,8},{20,12},{24,16},{28,20},{32,24... | collective-permute-start | bytes 393224 | tf_op jit(solution)/shard_map/ppermute | solution.py:17
  12.6 9.1 %shard_map.91 = (f32[72,512]{1,0:T(8,128)S(1)}, f32[32,128]{1,0:T(8,128)S(1)}, f32[32,128]{1,0:T(8,128)S(1)}, s32[8,128]{1,0:T(8,128)S(1)}) custom-call(s32[1,1]{1,0:T(1,128)} %bitcast.6.counts_ref, bf16[288,128]{1,0:T(8,128)(2,1)} %bitcast.13, f32[1,32]{1,0:T(1,128)} %bitcast.7, f32[1,32]{1,0:T(1,128)} %bitcast.10, bf16[128,64,512]{2,1,0:T(8,128)(2,1)} %refs_3_.1, ...), custom_call_target="tpu_custom_call" | custom-call | flops 8000000000 | bytes 9000000 | tf_op jit(solution)/shard_map/pallas_call | solution.py:163
  21.6 0.1 collective-permute-start.5
  21.8 0.0 copy-start
  21.8 0.0 copy-start.1
  21.8 3.1 %shard_map.93 = (f32[32,1536]{1,0:T(8,128)S(1)}, f32[32,1152]{1,0:T(8,128)S(1)}) custom-call(s32[4]{0:T(128)S(1)} %copy-done.5, s32[8,128]{1,0:T(8,128)S(1)} %get-tuple-element.21.counts_ref, f32[64,512]{1,0:T(8,128)S(1)} %copy-done.3, f32[64,512]{1,0:T(8,128)S(1)} %collective-permute-done.s1, f32[64,512]{1,0:T(8,128)S(1)} %collective-permute-done.1.s4, ...), custom_call_target="tpu_custom_call" | custom-call | flops 3000000000 | bytes 2000000 | tf_op jit(solution)/shard_map/pallas_call | solution.py:288
  25.0 0.1 collective-permute-start.4
  25.1 3.1 %shard_map.92 = (f32[32,1536]{1,0:T(8,128)S(1)}, f32[32,1024]{1,0:T(8,128)S(1)}) custom-call(s32[4]{0:T(128)S(1)} %copy-done.5, s32[8,128]{1,0:T(8,128)S(1)} %get-tuple-element.21.counts_ref, f32[64,512]{1,0:T(8,128)S(1)} %copy-done.3, f32[64,512]{1,0:T(8,128)S(1)} %collective-permute-done.s1, f32[64,512]{1,0:T(8,128)S(1)} %collective-permute-done.1.s4, ...), custom_call_target="tpu_custom_call" | custom-call | flops 3000000000 | bytes 2000000 | tf_op jit(solution)/shard_map/pallas_call | solution.py:288
  28.3 0.2 shard_map.94
  28.5 0.6 %collective-permute-start.6 = (f32[32,1024]{1,0:T(8,128)S(1)}, f32[32,1024]{1,0:T(8,128)S(1)}, u32[]{:S(2)}, u32[]{:S(2)}) collective-permute-start(f32[32,1024]{1,0:T(8,128)S(1)} %get-tuple-element.30), channel_id=1, source_target_pairs={{0,4},{4,0},{8,12},{12,8},{16,20},{20,16},{24,28},{28,24},{32,36},... | collective-permute-start | bytes 393224 | tf_op jit(solution)/shard_map/ppermute | solution.py:21
  29.1 2.3 %collective-permute-start.8 = (f32[16,1536]{1,0:T(8,128)S(1)}, f32[16,1536]{1,0:T(8,128)S(1)}, u32[]{:S(2)}, u32[]{:S(2)}) collective-permute-start(f32[16,1536]{1,0:T(8,128)S(1)} %get-tuple-element.29), channel_id=1, source_target_pairs={{0,2},{1,3},{2,0},{3,1},{4,6},{5,7},{6,4},{7,5},{8,10},{9,11},{10,... | collective-permute-start | bytes 294920 | tf_op jit(solution)/shard_map/ppermute | solution.py:21
  31.4 0.2 shard_map.95
  31.6 2.5 %collective-permute-start.7 = (f32[16,1536]{1,0:T(8,128)S(1)}, f32[16,1536]{1,0:T(8,128)S(1)}, u32[]{:S(2)}, u32[]{:S(2)}) collective-permute-start(f32[16,1536]{1,0:T(8,128)S(1)} %get-tuple-element.32), channel_id=1, source_target_pairs={{0,1},{1,0},{2,3},{3,2},{4,5},{5,4},{6,7},{7,6},{8,9},{9,8},{10,11... | collective-permute-start | bytes 294920 | tf_op jit(solution)/shard_map/ppermute | solution.py:21
  34.1 1.6 %collective-permute-done.8.c = f32[16,1536]{1,0:T(8,128)S(1)} collective-permute-done((f32[16,1536]{1,0:T(8,128)S(1)}, f32[16,1536]{1,0:T(8,128)S(1)}, u32[]{:S(2)}, u32[]{:S(2)}) %collective-permute-start.8) | collective-permute-done | bytes 98336 | tf_op jit(solution)/shard_map/ppermute | solution.py:21
  35.7 2.0 %collective-permute-done.9.d = f32[16,1536]{1,0:T(8,128)S(1)} collective-permute-done((f32[16,1536]{1,0:T(8,128)S(1)}, f32[16,1536]{1,0:T(8,128)S(1)}, u32[]{:S(2)}, u32[]{:S(2)}) %collective-permute-start.9) | collective-permute-done | bytes 98336 | tf_op jit(solution)/shard_map/ppermute | solution.py:21
  37.7 0.1 collective-permute-done.7.b
  37.8 1.7 %collective-permute-start.11 = (f32[16,512]{1,0:T(8,128)S(1)}, f32[16,512]{1,0:T(8,128)S(1)}, u32[]{:S(2)}, u32[]{:S(2)}) collective-permute-start(f32[16,512]{1,0:T(8,128)S(1)} %get-tuple-element.36), channel_id=1, source_target_pairs={{0,16},{4,20},{8,24},{12,28},{16,32},{20,36},{24,40},{28,44},{32,4... | collective-permute-start | bytes 98312 | tf_op jit(solution)/shard_map/ppermute | solution.py:17
  39.6 2.7 %collective-permute-start.10 = (f32[16,512]{1,0:T(8,128)S(1)}, f32[16,512]{1,0:T(8,128)S(1)}, u32[]{:S(2)}, u32[]{:S(2)}) collective-permute-start(f32[16,512]{1,0:T(8,128)S(1)} %get-tuple-element.35), channel_id=1, source_target_pairs={{0,8},{4,12},{8,16},{12,20},{16,24},{20,28},{24,32},{28,36},{32,40... | collective-permute-start | bytes 98312 | tf_op jit(solution)/shard_map/ppermute | solution.py:17
  42.3 3.5 %collective-permute-done.11 = f32[16,512]{1,0:T(8,128)S(1)} collective-permute-done((f32[16,512]{1,0:T(8,128)S(1)}, f32[16,512]{1,0:T(8,128)S(1)}, u32[]{:S(2)}, u32[]{:S(2)}) %collective-permute-start.11) | collective-permute-done | bytes 32800 | tf_op jit(solution)/shard_map/ppermute | solution.py:17
  45.8 1.0 %collective-permute-done.10 = f32[16,512]{1,0:T(8,128)S(1)} collective-permute-done((f32[16,512]{1,0:T(8,128)S(1)}, f32[16,512]{1,0:T(8,128)S(1)}, u32[]{:S(2)}, u32[]{:S(2)}) %collective-permute-start.10) | collective-permute-done | bytes 32800 | tf_op jit(solution)/shard_map/ppermute | solution.py:17
  46.8 0.6 %add_add_fusion = f32[16,512]{1,0:T(8,128)} fusion(f32[16,512]{1,0:T(8,128)S(1)} %collective-permute-done.11, f32[16,512]{1,0:T(8,128)S(1)} %get-tuple-element.34, f32[16,512]{1,0:T(8,128)S(1)} %collective-permute-done.10), kind=kLoop, calls=%fused_computation | loop fusion | flops 16384 | bytes 131072 | tf_op jit(solution)/shard_map/add | solution.py:385
  (19 shorter events, 0.1 us)
Async XLA Ops:
  0.0 21.7 %collective-permute-start = (f32[64,512]{1,0:T(8,128)}, f32[64,512]{1,0:T(8,128)S(1)}, u32[]{:S(2)}, u32[]{:S(2)}) collective-permute-start(f32[64,512]{1,0:T(8,128)} %s0.3), channel_id=1, source_target_pairs={{0,252},{4,0},{8,4},{12,8},{16,12},{20,16},{24,20},{28,24},{32,28}... | collective-permute-start | bytes 393224 | tf_op jit(solution)/shard_map/ppermute | solution.py:17
  7.5 14.2 %collective-permute-start.1 = (f32[64,512]{1,0:T(8,128)}, f32[64,512]{1,0:T(8,128)S(1)}, u32[]{:S(2)}, u32[]{:S(2)}) collective-permute-start(f32[64,512]{1,0:T(8,128)} %s0.3), channel_id=1, source_target_pairs={{0,240},{4,244},{8,248},{12,252},{16,0},{20,4},{24,8},{28,12},{32,... | collective-permute-start | bytes 393224 | tf_op jit(solution)/shard_map/ppermute | solution.py:17
  8.3 13.4 %collective-permute-start.2 = (f32[64,512]{1,0:T(8,128)}, f32[64,512]{1,0:T(8,128)S(1)}, u32[]{:S(2)}, u32[]{:S(2)}) collective-permute-start(f32[64,512]{1,0:T(8,128)} %s0.3), channel_id=1, source_target_pairs={{0,244},{4,248},{8,252},{12,0},{16,4},{20,8},{24,12},{28,16},{32,2... | collective-permute-start | bytes 393224 | tf_op jit(solution)/shard_map/ppermute | solution.py:17
  8.7 13.1 %collective-permute-start.3 = (f32[64,512]{1,0:T(8,128)}, f32[64,512]{1,0:T(8,128)S(1)}, u32[]{:S(2)}, u32[]{:S(2)}) collective-permute-start(f32[64,512]{1,0:T(8,128)} %s0.3), channel_id=1, source_target_pairs={{0,248},{4,252},{8,0},{12,4},{16,8},{20,12},{24,16},{28,20},{32,24... | collective-permute-start | bytes 393224 | tf_op jit(solution)/shard_map/ppermute | solution.py:17
  12.5 9.3 %copy-start.2 = (f32[4,64,2048]{2,1,0:T(8,128)S(1)}, f32[4,64,2048]{2,1,0:T(8,128)}, u32[]{:S(2)}) copy-start(f32[4,64,2048]{2,1,0:T(8,128)} %record_ref.3) | copy-start | bytes 6291460
  12.5 9.3 %copy-start.3 = (f32[64,512]{1,0:T(8,128)S(1)}, f32[64,512]{1,0:T(8,128)}, u32[]{:S(2)}) copy-start(f32[64,512]{1,0:T(8,128)} %s0.3) | copy-start | bytes 393220
  12.5 9.3 %copy-start.4 = (f32[4,256]{1,0:T(4,128)S(1)}, f32[4,256]{1,0:T(4,128)}, u32[]{:S(2)}) copy-start(f32[4,256]{1,0:T(4,128)} %taps_ref.3) | copy-start | bytes 12292
  12.5 9.3 %copy-start.5 = (s32[4]{0:T(128)S(1)}, s32[4]{0:T(128)}, u32[]{:S(2)}) copy-start(s32[4]{0:T(128)} %offsets_ref.3) | copy-start | bytes 52
  21.6 6.6 %collective-permute-start.5 = (f32[32,128]{1,0:T(8,128)S(1)}, f32[32,128]{1,0:T(8,128)S(1)}, u32[]{:S(2)}, u32[]{:S(2)}) collective-permute-start(f32[32,128]{1,0:T(8,128)S(1)} %get-tuple-element.22.send_ref), channel_id=1, source_target_pairs={{0,252},{4,8},{8,4},{12,16},{16,12},{20,24},{24,20},{28,32},{32,28... | collective-permute-start | bytes 49160 | tf_op jit(solution)/shard_map/ppermute | solution.py:365
  21.8 6.5 %copy-start = (f32[32]{0:T(128)S(1)}, f32[32]{0:T(128)}, u32[]{:S(2)}) copy-start(f32[32]{0:T(128)} %param.16) | copy-start | bytes 388
  21.8 6.5 %copy-start.1 = (f32[32]{0:T(128)S(1)}, f32[32]{0:T(128)}, u32[]{:S(2)}) copy-start(f32[32]{0:T(128)} %param.17) | copy-start | bytes 388
  25.0 3.3 %collective-permute-start.4 = (f32[32,1152]{1,0:T(8,128)S(1)}, f32[32,1152]{1,0:T(8,128)S(1)}, u32[]{:S(2)}, u32[]{:S(2)}) collective-permute-start(f32[32,1152]{1,0:T(8,128)S(1)} %get-tuple-element.26), channel_id=1, source_target_pairs={{0,4},{4,0},{8,12},{12,8},{16,20},{20,16},{24,28},{28,24},{32,36},... | collective-permute-start | bytes 442376 | tf_op jit(solution)/shard_map/ppermute | solution.py:21
  28.5 2.9 %collective-permute-start.6 = (f32[32,1024]{1,0:T(8,128)S(1)}, f32[32,1024]{1,0:T(8,128)S(1)}, u32[]{:S(2)}, u32[]{:S(2)}) collective-permute-start(f32[32,1024]{1,0:T(8,128)S(1)} %get-tuple-element.30), channel_id=1, source_target_pairs={{0,4},{4,0},{8,12},{12,8},{16,20},{20,16},{24,28},{28,24},{32,36},... | collective-permute-start | bytes 393224 | tf_op jit(solution)/shard_map/ppermute | solution.py:21
  29.1 6.6 %collective-permute-start.8 = (f32[16,1536]{1,0:T(8,128)S(1)}, f32[16,1536]{1,0:T(8,128)S(1)}, u32[]{:S(2)}, u32[]{:S(2)}) collective-permute-start(f32[16,1536]{1,0:T(8,128)S(1)} %get-tuple-element.29), channel_id=1, source_target_pairs={{0,2},{1,3},{2,0},{3,1},{4,6},{5,7},{6,4},{7,5},{8,10},{9,11},{10,... | collective-permute-start | bytes 294920 | tf_op jit(solution)/shard_map/ppermute | solution.py:21
  31.4 6.3 %collective-permute-start.9 = (f32[16,1536]{1,0:T(8,128)S(1)}, f32[16,1536]{1,0:T(8,128)S(1)}, u32[]{:S(2)}, u32[]{:S(2)}) collective-permute-start(f32[16,1536]{1,0:T(8,128)S(1)} %get-tuple-element.33), channel_id=1, source_target_pairs={{0,3},{1,2},{2,1},{3,0},{4,7},{5,6},{6,5},{7,4},{8,11},{9,10},{10,... | collective-permute-start | bytes 294920 | tf_op jit(solution)/shard_map/ppermute | solution.py:21
  31.6 6.2 %collective-permute-start.7 = (f32[16,1536]{1,0:T(8,128)S(1)}, f32[16,1536]{1,0:T(8,128)S(1)}, u32[]{:S(2)}, u32[]{:S(2)}) collective-permute-start(f32[16,1536]{1,0:T(8,128)S(1)} %get-tuple-element.32), channel_id=1, source_target_pairs={{0,1},{1,0},{2,3},{3,2},{4,5},{5,4},{6,7},{7,6},{8,9},{9,8},{10,11... | collective-permute-start | bytes 294920 | tf_op jit(solution)/shard_map/ppermute | solution.py:21
  37.8 8.0 %collective-permute-start.11 = (f32[16,512]{1,0:T(8,128)S(1)}, f32[16,512]{1,0:T(8,128)S(1)}, u32[]{:S(2)}, u32[]{:S(2)}) collective-permute-start(f32[16,512]{1,0:T(8,128)S(1)} %get-tuple-element.36), channel_id=1, source_target_pairs={{0,16},{4,20},{8,24},{12,28},{16,32},{20,36},{24,40},{28,44},{32,4... | collective-permute-start | bytes 98312 | tf_op jit(solution)/shard_map/ppermute | solution.py:17
  39.6 7.2 %collective-permute-start.10 = (f32[16,512]{1,0:T(8,128)S(1)}, f32[16,512]{1,0:T(8,128)S(1)}, u32[]{:S(2)}, u32[]{:S(2)}) collective-permute-start(f32[16,512]{1,0:T(8,128)S(1)} %get-tuple-element.35), channel_id=1, source_target_pairs={{0,8},{4,12},{8,16},{12,20},{16,24},{20,28},{24,32},{28,36},{32,40... | collective-permute-start | bytes 98312 | tf_op jit(solution)/shard_map/ppermute | solution.py:17
